TPU v7x, 128 devices: a whole 4x4x4 slice. The times are simulated.
128 devices in a mesh: blk: 8 (over z_lo, x), grp: 16 (over y, z_hi, core).
Axes of the slice: x: 4, y: 4, z: 4 (z_hi: 2, z_lo: 2; z = z_hi * 2 + z_lo), core: 2. Of those that a mesh axis runs over, the one named last changes fastest.
Arguments:
- a_blocks: bfloat16 [16, 192, 27, 96, 96], P('grp', 'blk'), may hold values from -0.125 to 0.125
- col_index: int32 [16, 192, 27], P('grp', 'blk'), may hold values from 0 to 191
- prolong: bfloat16 [16, 192, 2, 96, 96], P('grp', 'blk'), may hold values from -0.625 to 0.625
- target: int32 [16, 192, 108], P('grp', 'blk'), may hold values from 0 to 511
Outputs:
- coarse: float32 [16, 32, 96, 96], P('grp', 'blk')
All inputs are finite; a program needn't handle non-finite values.
Results may differ from a plain program's by a relative error of at most 0.0029.
Values may be sent and summed in bfloat16 or wider, within the bound.
A program may use at most 320 MiB of HBM per device.

v0:
```python
import math

import jax
import jax.numpy as jnp
from jax import lax
from jax.sharding import PartitionSpec as P

OWN = 4


def shards(a_blocks, col_index, prolong, target):
    rows = a_blocks.shape[1]
    nonzeros = a_blocks.shape[2]
    per_row = prolong.shape[2]
    width = a_blocks.shape[-1]
    groups = lax.axis_size("grp")
    members = lax.axis_size("blk")
    coarse_g = OWN * members
    slots = groups * coarse_g
    columns = col_index[0]
    init = jnp.zeros((rows, nonzeros, per_row, width, width), jnp.bfloat16)
    piece = lax.all_gather(prolong, "blk", axis=1, tiled=True)
    count = piece.shape[1]
    inside = (columns >= 0) & (columns < count)
    taken = jnp.take(piece[0], jnp.clip(columns, 0, count - 1), axis=0)
    chosen = jnp.where(inside[:, :, None, None, None], taken, init)
    step = math.gcd(rows, 4)
    a_rows = a_blocks[0]
    p_trans = jnp.swapaxes(prolong[0], -1, -2)
    t_rows = target[0]

    def one_block(total, index):
        low = index * step
        a_part = lax.dynamic_slice_in_dim(a_rows, low, step, 0)
        c_part = lax.dynamic_slice_in_dim(chosen, low, step, 0)
        p_part = lax.dynamic_slice_in_dim(p_trans, low, step, 0)
        t_part = lax.dynamic_slice_in_dim(t_rows, low, step, 0)
        product = jnp.einsum(
            "rkab,rkmbc->rkmac", a_part, c_part, preferred_element_type=jnp.float32
        ).astype(jnp.bfloat16)
        partial_value = jnp.einsum(
            "rnab,rkmbc->rnkmac", p_part, product, preferred_element_type=jnp.float32
        )
        partial_value = partial_value.reshape(-1, width, width)
        total = total + jax.ops.segment_sum(partial_value, t_part.reshape(-1), num_segments=slots)
        return (total, None)

    start_buf = jnp.zeros((slots, width, width), jnp.float32)
    buffer, _ = lax.scan(one_block, start_buf, jnp.arange(rows // step, dtype=jnp.int32))
    buffer = buffer.reshape(groups, coarse_g, width, width)
    received = lax.all_to_all(buffer, "grp", split_axis=0, concat_axis=0, tiled=True)
    summed = jnp.sum(received, axis=0)
    mine = lax.psum_scatter(summed, "blk", scatter_dimension=0, tiled=True)
    return mine[None]


def solution(mesh):
    return jax.shard_map(
        shards,
        mesh=mesh,
        in_specs=(
            P("grp", "blk", None, None, None),
            P("grp", "blk", None),
            P("grp", "blk", None, None, None),
            P("grp", "blk", None),
        ),
        out_specs=P("grp", "blk", None, None),
        check_vma=False,
    )
```

profile of v0, /device:TPU:0, one launch (start us, length us, event | category | flops | bytes accessed | tf_op | source)
XLA Modules:
  0.0 1215.8 jit_solution(3651651304745386798)
XLA Ops:
  6.5 0.7 all-gather.2.cloned.1.call-update
  7.3 1.7 copy.11
  9.0 0.7 compare_select_fusion
  9.7 0.1 reshape.60
  9.8 0.7 compare_and_fusion
  10.5 0.7 and_bitcast_fusion
  11.2 102.1 %all-gather.2.cloned.1.call-done = bf16[1,192,2,96,96]{4,3,2,0,1:T(8,128)(2,1)} async-done(((bf16[1,24,2,96,96]{4,3,2,0,1:T(8,128)(2,1)}), bf16[1,192,2,96,96]{4,3,2,0,1:T(8,128)(2,1)}) %all-gather.2.cloned.1.call-update) | async-done | bytes 7077904 | tf_op jit(solution)/shard_map/all_gather | solution.py:22
  113.3 24.5 %gather_fusion = bf16[648,2,96,96]{3,2,1,0:T(8,128)(2,1)} fusion(bf16[192,2,96,96]{3,2,1,0:T(8,128)(2,1)} %bitcast.57, s32[1024]{0:T(1024)S(1)} %pad_clamp_fusion), kind=kCustom, calls=%fused_computation | custom fusion | bytes 47778336 | tf_op jit(solution)/shard_map/jit(_take)/gather | solution.py:25
  137.8 38.4 %copy.10 = bf16[24,27,2,96,96]{3,4,2,1,0:T(8,128)(2,1)} copy(bf16[24,27,2,96,96]{4,3,2,1,0:T(8,128)(2,1)} %bitcast.56) | data formatting | bytes 47775744 | tf_op jit(solution)/shard_map/jit(_take)/gather | solution.py:25
  176.3 22.1 %select_select_fusion = bf16[24,27,2,96,96]{3,4,2,1,0:T(8,128)(2,1)} fusion(bf16[24,27,2,96,96]{3,4,2,1,0:T(8,128)(2,1)} %copy.10, pred[24,27]{1,0:T(8,128)(4,1)S(1)} %compare_and_fusion, pred[24,27]{1,0:T(8,128)(4,1)S(1)} %and_bitcast_fusion), kind=kLoop, calls=%fused_computation.13 | loop fusion | flops 23887872 | bytes 47777040 | tf_op jit(solution)/shard_map/jit(_where)/select_n | solution.py:26
  198.3 11.5 broadcast.65
  209.9 662.9 %while.10 = (s32[]{:T(128)}, f32[512,96,96]{2,1,0:T(8,128)}, s32[6]{0:T(128)S(1)}, s32[24,108]{1,0:T(8,128)}, bf16[24,27,2,96,96]{3,4,2,1,0:T(8,128)(2,1)}, /*in...) while((s32[]{:T(128)}, f32[512,96,96]{2,1,0:T(8,128)}, ...), condition=%wide.region_2.3_spmd, body=%wide.region_0.2_spmd.sunk | while | flops 1152589824 | bytes 103721072 | solution.py:49
  209.9 0.6 dynamic_slice.38
  211.1 0.7 constant_dynamic-slice_fusion.2
  211.9 11.6 convolution_bitcast_fusion.2
  223.5 21.1 %copy.16 = f32[4,2,27,2,96,96]{5,4,3,2,1,0:T(8,128)} copy(f32[4,2,27,2,96,96]{4,5,1,3,2,0:T(8,128)} %convolution_bitcast_fusion.2) | data formatting | bytes 31850496 | tf_op jit(solution)/shard_map/while/body/eval_jaxpr/rnab,rkmbc->rnkmac/transpose | solution.py:41
  244.6 75.7 %scatter_fusion = f32[512,96,96]{2,1,0:T(8,128)} fusion(f32[512,96,96]{2,1,0:T(8,128)} %get-tuple-element.112, s32[432]{0:T(512)S(1)} %reshape.84, f32[432,96,96]{2,1,0:T(8,128)} %bitcast.54), kind=kCustom, calls=%fused_computation.1.clone.1 | custom fusion | flops 3981312 | bytes 47777472 | tf_op jit(solution)/shard_map/while/body/eval_jaxpr/scatter-add | solution.py:45
  320.2 0.6 dynamic_slice.38
  321.5 0.7 constant_dynamic-slice_fusion.2
  322.2 11.6 convolution_bitcast_fusion.2
  333.9 21.1 %copy.16 = f32[4,2,27,2,96,96]{5,4,3,2,1,0:T(8,128)} copy(f32[4,2,27,2,96,96]{4,5,1,3,2,0:T(8,128)} %convolution_bitcast_fusion.2) | data formatting | bytes 31850496 | tf_op jit(solution)/shard_map/while/body/eval_jaxpr/rnab,rkmbc->rnkmac/transpose | solution.py:41
  354.9 75.6 %scatter_fusion = f32[512,96,96]{2,1,0:T(8,128)} fusion(f32[512,96,96]{2,1,0:T(8,128)} %get-tuple-element.112, s32[432]{0:T(512)S(1)} %reshape.84, f32[432,96,96]{2,1,0:T(8,128)} %bitcast.54), kind=kCustom, calls=%fused_computation.1.clone.1 | custom fusion | flops 3981312 | bytes 47777472 | tf_op jit(solution)/shard_map/while/body/eval_jaxpr/scatter-add | solution.py:45
  430.5 0.6 dynamic_slice.38
  431.7 0.7 constant_dynamic-slice_fusion.2
  432.4 0.1 reshape.84
  432.5 11.6 convolution_bitcast_fusion.2
  444.2 21.1 %copy.16 = f32[4,2,27,2,96,96]{5,4,3,2,1,0:T(8,128)} copy(f32[4,2,27,2,96,96]{4,5,1,3,2,0:T(8,128)} %convolution_bitcast_fusion.2) | data formatting | bytes 31850496 | tf_op jit(solution)/shard_map/while/body/eval_jaxpr/rnab,rkmbc->rnkmac/transpose | solution.py:41
  465.2 76.0 %scatter_fusion = f32[512,96,96]{2,1,0:T(8,128)} fusion(f32[512,96,96]{2,1,0:T(8,128)} %get-tuple-element.112, s32[432]{0:T(512)S(1)} %reshape.84, f32[432,96,96]{2,1,0:T(8,128)} %bitcast.54), kind=kCustom, calls=%fused_computation.1.clone.1 | custom fusion | flops 3981312 | bytes 47777472 | tf_op jit(solution)/shard_map/while/body/eval_jaxpr/scatter-add | solution.py:45
  541.2 0.6 dynamic_slice.38
  542.4 0.7 constant_dynamic-slice_fusion.2
  543.1 0.1 reshape.84
  543.2 11.6 convolution_bitcast_fusion.2
  554.8 21.1 %copy.16 = f32[4,2,27,2,96,96]{5,4,3,2,1,0:T(8,128)} copy(f32[4,2,27,2,96,96]{4,5,1,3,2,0:T(8,128)} %convolution_bitcast_fusion.2) | data formatting | bytes 31850496 | tf_op jit(solution)/shard_map/while/body/eval_jaxpr/rnab,rkmbc->rnkmac/transpose | solution.py:41
  575.9 75.9 %scatter_fusion = f32[512,96,96]{2,1,0:T(8,128)} fusion(f32[512,96,96]{2,1,0:T(8,128)} %get-tuple-element.112, s32[432]{0:T(512)S(1)} %reshape.84, f32[432,96,96]{2,1,0:T(8,128)} %bitcast.54), kind=kCustom, calls=%fused_computation.1.clone.1 | custom fusion | flops 3981312 | bytes 47777472 | tf_op jit(solution)/shard_map/while/body/eval_jaxpr/scatter-add | solution.py:45
  651.7 0.6 dynamic_slice.38
  653.0 0.7 constant_dynamic-slice_fusion.2
  653.7 0.1 reshape.84
  653.8 11.6 convolution_bitcast_fusion.2
  665.4 21.1 %copy.16 = f32[4,2,27,2,96,96]{5,4,3,2,1,0:T(8,128)} copy(f32[4,2,27,2,96,96]{4,5,1,3,2,0:T(8,128)} %convolution_bitcast_fusion.2) | data formatting | bytes 31850496 | tf_op jit(solution)/shard_map/while/body/eval_jaxpr/rnab,rkmbc->rnkmac/transpose | solution.py:41
  686.4 75.8 %scatter_fusion = f32[512,96,96]{2,1,0:T(8,128)} fusion(f32[512,96,96]{2,1,0:T(8,128)} %get-tuple-element.112, s32[432]{0:T(512)S(1)} %reshape.84, f32[432,96,96]{2,1,0:T(8,128)} %bitcast.54), kind=kCustom, calls=%fused_computation.1.clone.1 | custom fusion | flops 3981312 | bytes 47777472 | tf_op jit(solution)/shard_map/while/body/eval_jaxpr/scatter-add | solution.py:45
  762.2 0.6 dynamic_slice.38
  763.5 0.7 constant_dynamic-slice_fusion.2
  764.2 11.6 convolution_bitcast_fusion.2
  775.9 21.1 %copy.16 = f32[4,2,27,2,96,96]{5,4,3,2,1,0:T(8,128)} copy(f32[4,2,27,2,96,96]{4,5,1,3,2,0:T(8,128)} %convolution_bitcast_fusion.2) | data formatting | bytes 31850496 | tf_op jit(solution)/shard_map/while/body/eval_jaxpr/rnab,rkmbc->rnkmac/transpose | solution.py:41
  796.9 75.8 %scatter_fusion = f32[512,96,96]{2,1,0:T(8,128)} fusion(f32[512,96,96]{2,1,0:T(8,128)} %get-tuple-element.112, s32[432]{0:T(512)S(1)} %reshape.84, f32[432,96,96]{2,1,0:T(8,128)} %bitcast.54), kind=kCustom, calls=%fused_computation.1.clone.1 | custom fusion | flops 3981312 | bytes 47777472 | tf_op jit(solution)/shard_map/while/body/eval_jaxpr/scatter-add | solution.py:45
  872.7 284.9 %all_to_all.5 = f32[16,32,96,96]{3,2,1,0:T(8,128)} all-to-all(f32[16,32,96,96]{3,2,1,0:T(8,128)} %bitcast.55), channel_id=1, replica_groups=mesh['blk'=8,'grp'=16] {'grp'}, dimensions={0} | all-to-all | bytes 37748736 | tf_op jit(solution)/shard_map/all_to_all | solution.py:51
  1157.6 11.4 reduce_sum.9
  1169.1 39.9 %reduce-scatter.2.cloned.1.call-done = f32[4,96,96]{2,1,0:T(8,128)} async-done(((f32[32,96,96]{2,1,0:T(8,128)}), f32[4,96,96]{2,1,0:T(8,128)}) %reduce-scatter.2.cloned.1.call-update) | async-done | bytes 147472 | tf_op jit(solution)/shard_map/reduce_scatter | solution.py:53
  (8 shorter events, 0.3 us)
Async XLA Ops:
  6.5 106.8 %all-gather.2.cloned.1.call-start = ((), (), s32[]{:S(2)}) async-start(), calls=%async_computation.2 | async-start | bytes 10616832 | tf_op jit(solution)/shard_map/all_gather | solution.py:22
  7.3 1201.7 %reduce-scatter.2.cloned.1.call-start = ((), (), s32[]{:S(2)}) async-start(), calls=%async_computation.3 | async-start | bytes 1769472 | tf_op jit(solution)/shard_map/reduce_scatter | solution.py:53
Sparse Core Ops, SparseCore 0:
  9.0 104.2 all-gather.1
  1169.2 39.7 reduce-scatter.1
where the time goes:
time: 1220 us
  other arithmetic  490 us (40%)
  blocking collectives  285 us (23%)
  local copies, waits for them, and re-layouts  211 us (17%)
  waiting for transfers between devices  143 us (12%)
  matrix products  69.8 us (6%)
  between operations  13.4 us (1%)
    scatter-add x6, other arithmetic, one_block(): jax.ops.segment_sum(partial_value, t_part.reshape(-1), num_segments=slots)  455 us
    all_to_all x1, blocking collectives, shards(): lax.all_to_all(buffer, 'grp', split_axis=0, concat_axis=0, tiled=True)  285 us
    transpose x6, local copies, waits for them, and re-layouts, one_block(): jnp.einsum('rnab,rkmbc->rnkmac', p_part, product, preferred_element_type=...  126 us
    all_gather x1, waiting for transfers between devices, shards(): piece = lax.all_gather(prolong, 'blk', axis=1, tiled=True)  102 us
    dot_general x6, matrix products, one_block(): jnp.einsum('rnab,rkmbc->rnkmac', p_part, product, preferred_element_type=...  69.8 us
    gather x2, local copies, waits for them, and re-layouts, shards(): taken = jnp.take(piece[0], jnp.clip(columns, 0, count - 1), axis=0)  62.9 us
    reduce_scatter x1, waiting for transfers between devices, shards(): mine = lax.psum_scatter(summed, 'blk', scatter_dimension=0, tiled=True)  39.9 us
  transfers between devices with their start and end apart: 2, of which 2 were waited for; matrix products, arithmetic and copies ran while one was open for 0% of the time, Pallas kernels for 0%

commit v1 on v0

v1 whole, which is shorter than its diff:
```python
import functools

import jax
import jax.numpy as jnp
from jax import lax
from jax.experimental import pallas as pl
from jax.experimental.pallas import tpu as pltpu
from jax.sharding import PartitionSpec as P

f32, bf16 = jnp.float32, jnp.bfloat16
MESH = pl.DeviceIdType.MESH

B = 96
LANES = 128
PACK = 72
KP = 2
KA = 27
FR = 24
MEMBERS = 8
GROUPS = 16
OWN = 4
SLOTS = 512
PARTS = 6
PIECE = OWN * PACK // PARTS
STEPS = 6
WIDE_FROM = 2

BITS = ("xg", "yg", "zg", "xh", "yh", "zh")


def bits_of(grp, blk):
    x, zl = blk % 4, blk // 4
    y, zh, core = grp // 4, (grp // 2) % 2, grp % 2
    xh, yh = x // 2, y // 2
    return {
        "xg": (xh + x % 2) % 2, "yg": (yh + y % 2) % 2, "zg": (zh + zl) % 2,
        "xh": xh, "yh": yh, "zh": zh, "core": core,
    }


def partner_of(grp, blk, bit):
    x, zl = blk % 4, blk // 4
    y, zh, core = grp // 4, (grp // 2) % 2, grp % 2
    if bit == "xg":
        x = x + 1 - 2 * (x % 2)
    elif bit == "xh":
        x = 3 - x
    elif bit == "yg":
        y = y + 1 - 2 * (y % 2)
    elif bit == "yh":
        y = 3 - y
    elif bit in ("zg", "zl"):
        zl = 1 - zl
    elif bit == "zh":
        zl, zh = 1 - zl, 1 - zh
    elif bit == "core":
        core = 1 - core
    return {"blk": zl * 4 + x, "grp": y * 4 + zh * 2 + core}


def order_of(part):
    return [BITS[(part + step) % STEPS] for step in range(STEPS)]


def enter(partners):
    barrier = pltpu.get_barrier_semaphore()
    for device in partners:
        pl.semaphore_signal(barrier, inc=1, device_id=device, device_id_type=MESH)
    pl.semaphore_wait(barrier, len(partners))


def fold(main, tail):
    lane = lax.broadcasted_iota(jnp.int32, main.shape, 1)
    side = jnp.concatenate([pltpu.roll(tail, shift, 1) for shift in (96, 64, 32)], axis=0)
    return jnp.where(lane < B, main, side)


def unfold(packed):
    n = packed.shape[0] // 3
    lane = lax.broadcasted_iota(jnp.int32, (n, LANES), 1)
    first = pltpu.roll(packed[:n], 32, 1)
    second = pltpu.roll(packed[n:2 * n], 64, 1)
    third = pltpu.roll(packed[2 * n:], 96, 1)
    return jnp.where(lane < 32, first, jnp.where(lane < 64, second, third))


G_ORDERS = (("xg", "xh", "zl"), ("xh", "zl", "xg"), ("zl", "xg", "xh"))
G_ROWS = FR // 3


def member_index(part, blk):
    x, zl = blk % 4, blk // 4
    xh = x // 2
    bits = {"xg": (xh + x % 2) % 2, "xh": xh, "zl": zl}
    return sum(bits[bit] * (1 << i) for i, bit in enumerate(G_ORDERS[part]))


def gather_kernel(p_ref, out_ref, mine, local_sem, send_sem, recv_sem):
    grp, blk = lax.axis_index("grp"), lax.axis_index("blk")
    partners = {bit: partner_of(grp, blk, bit) for bit in G_ORDERS[0]}
    for part in range(3):
        def pack(r, _):
            v = p_ref[part * G_ROWS + r].astype(f32)
            v = jnp.pad(v.reshape(KP * B, B), ((0, 0), (0, LANES - B)))
            mine[part, r] = fold(v[:2 * PACK], v[2 * PACK:]).astype(bf16)
            return 0
        lax.fori_loop(0, G_ROWS, pack, 0)
    enter(list(partners.values()))
    index = [member_index(part, blk) for part in range(3)]
    local = []
    for part in range(3):
        copy = pltpu.make_async_copy(mine.at[part], out_ref.at[part, index[part]], local_sem.at[part])
        copy.start()
        local.append(copy)
    sends = []
    for step in range(3):
        size = 1 << step
        current = []
        for part in range(3):
            if step == 1:
                local[part].wait()
            base = index[part] // size * size
            block = out_ref.at[part, pl.ds(base, size)]
            copy = pltpu.make_async_remote_copy(
                src_ref=mine.at[pl.ds(part, 1)] if step == 0 else block,
                dst_ref=block,
                send_sem=send_sem.at[step, part], recv_sem=recv_sem.at[step, part],
                device_id=partners[G_ORDERS[part][step]], device_id_type=MESH)
            if step:
                sends[-3].wait_recv()
            copy.start()
            sends.append(copy)
    for copy in sends[-3:]:
        copy.wait_recv()
    for copy in sends:
        copy.wait_send()


def gather(prolong):
    return pl.pallas_call(
        gather_kernel,
        out_shape=jax.ShapeDtypeStruct((3, MEMBERS, G_ROWS, 2 * PACK, LANES), bf16),
        in_specs=[pl.BlockSpec(memory_space=pltpu.VMEM)],
        out_specs=pl.BlockSpec(memory_space=pl.ANY),
        scratch_shapes=[
            pltpu.VMEM((3, G_ROWS, 2 * PACK, LANES), bf16),
            pltpu.SemaphoreType.DMA((3,)), pltpu.SemaphoreType.DMA((3, 3)), pltpu.SemaphoreType.DMA((3, 3))],
        compiler_params=pltpu.CompilerParams(collective_id=0, has_side_effects=True, vmem_limit_bytes=32 << 20),
        name="gather_prolong",
    )(prolong)


def product_kernel(col, tgt, a_ref, p_ref, g_ref, out_ref, raw, chosen, acc, p_trans, stage, g_sem, out_sem):
    i = pl.program_id(0)

    @pl.when(i == 0)
    def _():
        copies = [
            [pltpu.make_async_copy(g_ref.at[part, m], raw.at[part, m], g_sem.at[part, m]) for m in range(MEMBERS)]
            for part in range(3)]
        for row in copies:
            for copy in row:
                copy.start()

        @pl.loop(0, SLOTS)
        def _(s):
            acc[s] = jnp.zeros((B, LANES), f32)

        for part in range(3):
            for blk in range(MEMBERS):
                m = member_index(part, blk)
                copies[part][m].wait()

                def unpack(r, _):
                    packed = raw[part, m, r].astype(f32)
                    both = jnp.concatenate([packed, unfold(packed)], axis=0)
                    row = blk * FR + part * G_ROWS + r
                    for n in range(KP):
                        chosen[row, :, n * LANES:(n + 1) * LANES] = both[n * B:(n + 1) * B].astype(bf16)
                    return 0
                lax.fori_loop(0, G_ROWS, unpack, 0)

    for n in range(KP):
        p_trans[n * B:(n + 1) * B, :] = p_ref[0, n].T
    pt = p_trans[...]
    for k in range(KA):
        c = chosen[col[i * KA + k]]
        ap = jnp.dot(a_ref[0, k], c, preferred_element_type=f32).astype(bf16)
        value = jnp.dot(pt, ap, preferred_element_type=f32)
        for n in range(KP):
            for m in range(KP):
                slot = tgt[i * (KP * KA * KP) + n * (KA * KP) + k * KP + m]
                acc[slot] += value[n * B:(n + 1) * B, m * LANES:(m + 1) * LANES]

    @pl.when(i == pl.num_programs(0) - 1)
    def _():
        def flush(d, _):
            bits = bits_of(d // MEMBERS, d % MEMBERS)
            for pair in range(2):
                packed = []
                for j in range(2):
                    block = acc[d * OWN + pair * 2 + j]
                    packed.append(fold(block[:PACK], block[PACK:]))
                both = jnp.concatenate(packed, axis=0).astype(bf16)
                for piece in range(3):
                    part = pair * 3 + piece
                    entry = 0
                    for bit in order_of(part):
                        entry = entry * 2 + bits[bit]
                    stage[part, bits["core"], entry] = both[piece * PIECE:(piece + 1) * PIECE]
            return 0
        lax.fori_loop(0, GROUPS * MEMBERS, flush, 0)
        copy = pltpu.make_async_copy(stage, out_ref, out_sem)
        copy.start()
        copy.wait()


def products(a_rows, columns, p_rows, gathered, targets):
    stage = (PARTS, 2, 64, PIECE, LANES)
    return pl.pallas_call(
        product_kernel,
        out_shape=jax.ShapeDtypeStruct(stage, bf16),
        grid_spec=pltpu.PrefetchScalarGridSpec(
            num_scalar_prefetch=2, grid=(FR,),
            in_specs=[
                pl.BlockSpec((1, KA, B, B), lambda i, *_: (i, 0, 0, 0)),
                pl.BlockSpec((1, KP, B, B), lambda i, *_: (i, 0, 0, 0)),
                pl.BlockSpec(memory_space=pl.ANY)],
            out_specs=pl.BlockSpec(memory_space=pl.ANY),
            scratch_shapes=[
                pltpu.VMEM((3, MEMBERS, G_ROWS, 2 * PACK, LANES), bf16),
                pltpu.VMEM((FR * MEMBERS, B, KP * LANES), bf16),
                pltpu.VMEM((SLOTS, B, LANES), f32),
                pltpu.VMEM((KP * B, B), bf16),
                pltpu.VMEM(stage, bf16),
                pltpu.SemaphoreType.DMA((3, MEMBERS)), pltpu.SemaphoreType.DMA]),
        compiler_params=pltpu.CompilerParams(vmem_limit_bytes=60 << 20),
        name="products",
    )(columns.reshape(-1), targets.reshape(-1), a_rows, p_rows, gathered)


def wire(step):
    return f32 if step >= WIDE_FROM else bf16


def scatter_kernel(in_ref, out_ref, *refs):
    refs = list(refs)
    own, other = refs.pop(0), refs.pop(0)
    keep = [refs.pop(0) for _ in range(STEPS)]
    give = [refs.pop(0) for _ in range(STEPS)]
    got = [refs.pop(0) for _ in range(STEPS)]
    own_sem, core_send, core_recv, send_sem, recv_sem = refs
    grp, blk = lax.axis_index("grp"), lax.axis_index("blk")
    bits = bits_of(grp, blk)
    partners = {bit: partner_of(grp, blk, bit) for bit in BITS + ("core",)}
    core = bits["core"]
    local = []
    for part in range(PARTS):
        copy = pltpu.make_async_copy(in_ref.at[part, core], own.at[part], own_sem.at[part])
        copy.start()
        local.append(copy)
    enter(list(partners.values()))
    crossed = []
    for part in range(PARTS):
        copy = pltpu.make_async_remote_copy(
            src_ref=in_ref.at[part, 1 - core], dst_ref=other.at[part],
            send_sem=core_send.at[part], recv_sem=core_recv.at[part],
            device_id=partners["core"], device_id_type=MESH)
        copy.start()
        crossed.append(copy)
    sends = [[None] * PARTS for _ in range(STEPS)]
    for step in range(STEPS):
        half = 32 >> step
        for part in range(PARTS):
            bit = order_of(part)[step]
            away, here = (1 - bits[bit]) * half, bits[bit] * half
            if step == 0:
                local[part].wait()
                crossed[part].wait_recv()
                first, second = own, other
            else:
                sends[step - 1][part].wait_recv()
                first, second = keep[step - 1], got[step - 1]

            def combine(offset, target, dtype):
                def one(e, _):
                    total = first[part, offset + e].astype(f32) + second[part, offset + e].astype(f32)
                    target[part, e] = total.astype(dtype)
                    return 0
                lax.fori_loop(0, half, one, 0)

            combine(away, give[step], wire(step))
            copy = pltpu.make_async_remote_copy(
                src_ref=give[step].at[part], dst_ref=got[step].at[part],
                send_sem=send_sem.at[step, part], recv_sem=recv_sem.at[step, part],
                device_id=partners[bit], device_id_type=MESH)
            copy.start()
            sends[step][part] = copy
            combine(here, keep[step], f32)
    pieces = []
    for part in range(PARTS):
        sends[-1][part].wait_recv()
        pieces.append(keep[-1][part, 0] + got[-1][part, 0])
    for pair in range(2):
        both = jnp.concatenate(pieces[pair * 3:pair * 3 + 3], axis=0)
        for j in range(2):
            packed = both[j * PACK:(j + 1) * PACK]
            out_ref[0, pair * 2 + j, :PACK] = packed[:, :B]
            out_ref[0, pair * 2 + j, PACK:] = unfold(packed)[:, :B]
    for copy in crossed:
        copy.wait_send()
    for row in sends:
        for copy in row:
            copy.wait_send()


def scatter(staged):
    halves = [32 >> step for step in range(STEPS)]
    return pl.pallas_call(
        scatter_kernel,
        out_shape=jax.ShapeDtypeStruct((1, OWN, B, B), f32),
        in_specs=[pl.BlockSpec(memory_space=pl.ANY)],
        out_specs=pl.BlockSpec(memory_space=pltpu.VMEM),
        scratch_shapes=(
            [pltpu.VMEM((PARTS, 64, PIECE, LANES), bf16)] * 2
            + [pltpu.VMEM((PARTS, n, PIECE, LANES), f32) for n in halves]
            + [pltpu.VMEM((PARTS, n, PIECE, LANES), wire(s)) for s, n in enumerate(halves)] * 2
            + [pltpu.SemaphoreType.DMA((PARTS,))] * 3
            + [pltpu.SemaphoreType.DMA((STEPS, PARTS))] * 2),
        compiler_params=pltpu.CompilerParams(collective_id=1, has_side_effects=True, vmem_limit_bytes=48 << 20),
        name="sum_at_owners",
    )(staged)


def shards(a_blocks, col_index, prolong, target):
    gathered = gather(prolong[0])
    staged = products(a_blocks[0], col_index[0], prolong[0], gathered, target[0])
    return scatter(staged)


def solution(mesh):
    return jax.shard_map(
        shards,
        mesh=mesh,
        in_specs=(
            P("grp", "blk", None, None, None),
            P("grp", "blk", None),
            P("grp", "blk", None, None, None),
            P("grp", "blk", None),
        ),
        out_specs=P("grp", "blk", None, None),
        check_vma=False,
    )
```

time: 1220 us -> 216 us (0.18)
  other arithmetic: 490 us -> 0 us
  blocking collectives: 285 us -> 0 us
  Pallas kernels: 0 us -> 208 us
  local copies, waits for them, and re-layouts: 211 us -> 7.55 us
  waiting for transfers between devices: 143 us -> 0 us
  matrix products: 69.8 us -> 0 us
  between operations: 13.4 us -> 0.04 us
    scatter-add x6 -> x0, other arithmetic: 455 us -> none  [one_block(): jax.ops.segment_sum(partial_value, t_part.reshape(-1), num_segments=slots)]
    all_to_all x1 -> x0, blocking collectives: 285 us -> none  [shards(): lax.all_to_all(buffer, 'grp', split_axis=0, concat_axis=0, tiled=True)]
    pallas_call x0 -> x3, Pallas kernels: none -> 208 us  [the longest x1 108 us: products(): pl.pallas_call(product_kernel, out_shape=jax.ShapeDtypeStruct(stage, bf16...]
    transpose x6 -> x0, local copies, waits for them, and re-layouts: 126 us -> none  [one_block(): jnp.einsum('rnab,rkmbc->rnkmac', p_part, product, preferred_element_type=...]
    all_gather x1 -> x0, waiting for transfers between devices: 102 us -> none  [shards(): piece = lax.all_gather(prolong, 'blk', axis=1, tiled=True)]
    dot_general x6 -> x0, matrix products: 69.8 us -> none  [one_block(): jnp.einsum('rnab,rkmbc->rnkmac', p_part, product, preferred_element_type=...]
    gather x2 -> x0, local copies, waits for them, and re-layouts: 62.9 us -> none  [shards(): taken = jnp.take(piece[0], jnp.clip(columns, 0, count - 1), axis=0)]
    reduce_scatter x1 -> x0, waiting for transfers between devices: 39.9 us -> none  [shards(): mine = lax.psum_scatter(summed, 'blk', scatter_dimension=0, tiled=True)]
  transfers between devices with their start and end apart: 2 -> 0, of which waited for: 2 -> 0; matrix products, arithmetic and copies ran while one was open for 0% -> 0% of each run, Pallas kernels for 0% -> 0%
where the time goes in v1:
time: 216 us; the launch traced here: 215 us
  Pallas kernels  208 us (96%)
  local copies, waits for them, and re-layouts  7.55 us (3%)
    pallas_call x1, Pallas kernels, products(): pl.pallas_call(product_kernel, out_shape=jax.ShapeDtypeStruct(stage, bf16...  108 us
    pallas_call x1, Pallas kernels, gather(): pl.pallas_call(gather_kernel, out_shape=jax.ShapeDtypeStruct((3, MEMBERS,...  54 us
    pallas_call x1, Pallas kernels, scatter(): pl.pallas_call(scatter_kernel, out_shape=jax.ShapeDtypeStruct((1, OWN, B,...  45.6 us
    unnamed x5, local copies, waits for them, and re-layouts  4.77 us

profile of v1, /device:TPU:0, one launch (start us, length us, event | category | flops | bytes accessed | tf_op | source)
XLA Modules:
  0.0 215.4 jit_solution(13388943136717692244)
XLA Ops:
  0.0 1.4 reshape_squeeze.6.col
  1.4 1.4 reshape_squeeze.7.tgt
  2.8 0.0 copy-start.1
  2.8 1.3 copy-done.1
  4.0 54.0 %gather_prolong.1.g_ref = bf16[3,8,8,144,128]{4,3,2,1,0:T(8,128)(2,1)S(1)} custom-call(bf16[24,2,96,96]{3,2,1,0:T(8,128)(2,1)S(1)} %bitcast.3), custom_call_target="tpu_custom_call" | custom-call | tf_op jit(solution)/shard_map/gather_prolong/pallas_call | solution.py:140
  58.0 0.0 copy-start
  58.1 2.8 %copy-done = bf16[3,8,8,144,128]{4,3,2,1,0:T(8,128)(2,1)} copy-done((bf16[3,8,8,144,128]{4,3,2,1,0:T(8,128)(2,1)}, bf16[3,8,8,144,128]{4,3,2,1,0:T(8,128)(2,1)S(1)}, u32[]{:S(2)}) %copy-start) | copy-done | bytes 7077912
  60.9 108.3 %products.1.in_ref = bf16[6,2,64,48,128]{4,3,2,1,0:T(8,128)(2,1)} custom-call(s32[648]{0:T(1024)} %reshape_squeeze.6.col, s32[2592]{0:T(1024)} %reshape_squeeze.7.tgt, bf16[24,27,96,96]{3,2,1,0:T(8,128)(2,1)} %bitcast.4, bf16[24,2,96,96]{3,2,1,0:T(8,128)(2,1)} %bitcast.2, bf16[3,8,8,144,128]{4,3,2,1,0:T(8,128)(2,1)} %copy-done), custom_call_target="tpu_custom_call" | custom-call | tf_op jit(solution)/shard_map/products/pallas_call | solution.py:220
  169.2 45.6 %sum_at_owners.1 = f32[1,4,96,96]{3,2,1,0:T(8,128)S(1)} custom-call(bf16[6,2,64,48,128]{4,3,2,1,0:T(8,128)(2,1)} %products.1.in_ref), custom_call_target="tpu_custom_call" | custom-call | tf_op jit(solution)/shard_map/sum_at_owners/pallas_call | solution.py:319
  214.8 0.7 copy.6
Async XLA Ops:
  2.8 1.3 copy-start.1
  58.0 2.8 %copy-start = (bf16[3,8,8,144,128]{4,3,2,1,0:T(8,128)(2,1)}, bf16[3,8,8,144,128]{4,3,2,1,0:T(8,128)(2,1)S(1)}, u32[]{:S(2)}) copy-start(bf16[3,8,8,144,128]{4,3,2,1,0:T(8,128)(2,1)S(1)} %gather_prolong.1.g_ref) | copy-start | bytes 21233668

commit v2 on v1

v2 whole, which is shorter than its diff:
```python
import functools

import jax
import jax.numpy as jnp
from jax import lax
from jax.experimental import pallas as pl
from jax.experimental.pallas import tpu as pltpu
from jax.sharding import PartitionSpec as P

f32, bf16 = jnp.float32, jnp.bfloat16
MESH = pl.DeviceIdType.MESH

B = 96
LANES = 128
PACK = 72
KP = 2
KA = 27
FR = 24
MEMBERS = 8
GROUPS = 16
OWN = 4
SLOTS = 512
PARTS = 6
PIECE = OWN * PACK // PARTS
STEPS = 6
WIDE_FROM = 2

BITS = ("xg", "yg", "zg", "xh", "yh", "zh")


def bits_of(grp, blk):
    x, zl = blk % 4, blk // 4
    y, zh, core = grp // 4, (grp // 2) % 2, grp % 2
    xh, yh = x // 2, y // 2
    return {
        "xg": (xh + x % 2) % 2, "yg": (yh + y % 2) % 2, "zg": (zh + zl) % 2,
        "xh": xh, "yh": yh, "zh": zh, "core": core,
    }


def partner_of(grp, blk, bit):
    x, zl = blk % 4, blk // 4
    y, zh, core = grp // 4, (grp // 2) % 2, grp % 2
    if bit == "xg":
        x = x + 1 - 2 * (x % 2)
    elif bit == "xh":
        x = 3 - x
    elif bit == "yg":
        y = y + 1 - 2 * (y % 2)
    elif bit == "yh":
        y = 3 - y
    elif bit in ("zg", "zl"):
        zl = 1 - zl
    elif bit == "zh":
        zl, zh = 1 - zl, 1 - zh
    elif bit == "core":
        core = 1 - core
    return {"blk": zl * 4 + x, "grp": y * 4 + zh * 2 + core}


def order_of(part):
    return [BITS[(part + step) % STEPS] for step in range(STEPS)]


def slot_of(target):
    owner = target // OWN
    bits = bits_of(owner // MEMBERS, owner % MEMBERS)
    index = bits["core"]
    for bit in BITS:
        index = index * 2 + bits[bit]
    return index * OWN + target % OWN


def enter(partners):
    barrier = pltpu.get_barrier_semaphore()
    for device in partners:
        pl.semaphore_signal(barrier, inc=1, device_id=device, device_id_type=MESH)
    pl.semaphore_wait(barrier, len(partners))


def fold(main, tail):
    lane = lax.broadcasted_iota(jnp.int32, main.shape, 1)
    side = jnp.concatenate([pltpu.roll(tail, shift, 1) for shift in (96, 64, 32)], axis=0)
    return jnp.where(lane < B, main, side)


def unfold(packed):
    n = packed.shape[0] // 3
    lane = lax.broadcasted_iota(jnp.int32, (n, LANES), 1)
    first = pltpu.roll(packed[:n], 32, 1)
    second = pltpu.roll(packed[n:2 * n], 64, 1)
    third = pltpu.roll(packed[2 * n:], 96, 1)
    return jnp.where(lane < 32, first, jnp.where(lane < 64, second, third))


G_ORDERS = (("xg", "xh", "zl"), ("xh", "zl", "xg"), ("zl", "xg", "xh"))
G_PARTS = 3
G_ROWS = FR // G_PARTS


def member(part, blk, flip):
    x, zl = blk % 4, blk // 4
    xh = x // 2
    bits = {"xg": (xh + x % 2) % 2, "xh": xh, "zl": zl}
    index = 0
    for i, bit in enumerate(G_ORDERS[part]):
        if flip >> i & 1:
            bits[bit] = 1 - bits[bit]
        index = index + bits[bit] * (1 << i)
    return index, bits["zl"] * 4 + bits["xh"] * 2 + (bits["xh"] + bits["xg"]) % 2


def gather_kernel(p_ref, out_ref, landed, send_sem, recv_sem):
    grp, blk = lax.axis_index("grp"), lax.axis_index("blk")
    partners = {bit: partner_of(grp, blk, bit) for bit in G_ORDERS[0]}
    where = [[member(part, blk, flip) for flip in range(MEMBERS)] for part in range(G_PARTS)]
    for part in range(G_PARTS):
        mine = where[part][0][0]

        def pack(r, _):
            v = p_ref[part * G_ROWS + r].astype(f32)
            v = jnp.pad(v.reshape(KP * B, B), ((0, 0), (0, LANES - B)))
            landed[part, mine, r] = fold(v[:KP * PACK], v[KP * PACK:]).astype(bf16)
            return 0
        lax.fori_loop(0, G_ROWS, pack, 0, unroll=True)
    enter(list(partners.values()))
    sends = []
    arrivals = {}

    def forward(part, flip, step):
        index = where[part][flip][0]
        copy = pltpu.make_async_remote_copy(
            src_ref=landed.at[part, index], dst_ref=landed.at[part, index],
            send_sem=send_sem.at[part, (1 << step) - 1 + flip], recv_sem=recv_sem.at[part, (1 << step) + flip],
            device_id=partners[G_ORDERS[part][step]], device_id_type=MESH)
        copy.start()
        sends.append(copy)
        arrivals[part, (1 << step) + flip] = copy

    def unpack(part, flip):
        index, source = where[part][flip]

        def one(r, _):
            packed = landed[part, index, r]
            both = jnp.concatenate([packed, unfold(packed)], axis=0)
            row = source * FR + part * G_ROWS + r
            for n in range(KP):
                out_ref[row, :, n * LANES:(n + 1) * LANES] = both[n * B:(n + 1) * B]
            return 0
        lax.fori_loop(0, G_ROWS, one, 0, unroll=True)

    for step in range(3):
        for part in range(G_PARTS):
            forward(part, 0, step)
    for part in range(G_PARTS):
        unpack(part, 0)
    for flip in range(1, MEMBERS):
        for part in range(G_PARTS):
            arrivals[part, flip].wait_recv()
            for step in range(flip.bit_length(), 3):
                forward(part, flip, step)
        for part in range(G_PARTS):
            unpack(part, flip)
    for copy in sends:
        copy.wait_send()


def gather(prolong):
    return pl.pallas_call(
        gather_kernel,
        out_shape=jax.ShapeDtypeStruct((FR * MEMBERS, B, KP * LANES), bf16),
        in_specs=[pl.BlockSpec(memory_space=pltpu.VMEM)],
        out_specs=pl.BlockSpec(memory_space=pltpu.VMEM),
        scratch_shapes=[
            pltpu.VMEM((G_PARTS, MEMBERS, G_ROWS, KP * PACK, LANES), bf16),
            pltpu.SemaphoreType.DMA((G_PARTS, MEMBERS)), pltpu.SemaphoreType.DMA((G_PARTS, MEMBERS))],
        compiler_params=pltpu.CompilerParams(collective_id=0, has_side_effects=True, vmem_limit_bytes=20 << 20),
        name="gather_prolong",
    )(prolong)


A_SLOTS = 3


def product_kernel(col, tgt, a_ref, p_ref, chosen, acc, a_buf, p_trans, a_sem):
    def fetch(i):
        slot = i % A_SLOTS
        return pltpu.make_async_copy(a_ref.at[i], a_buf.at[slot], a_sem.at[slot])

    for i in range(A_SLOTS - 1):
        fetch(i).start()

    @pl.loop(0, SLOTS // 8)
    def _(s):
        for j in range(8):
            acc[s * 8 + j] = jnp.zeros((B, LANES), f32)

    @pl.loop(0, FR)
    def _(i):
        for n in range(KP):
            p_trans[n * B:(n + 1) * B, :] = p_ref[i, n].T
        pt = p_trans[...]
        fetch(i).wait()

        @pl.when(i + A_SLOTS - 1 < FR)
        def _():
            fetch(i + A_SLOTS - 1).start()

        a = a_buf.at[i % A_SLOTS]
        aps = [jnp.dot(a[k], chosen[col[i * KA + k]], preferred_element_type=f32).astype(bf16) for k in range(KA)]
        values = [jnp.dot(pt, ap, preferred_element_type=f32) for ap in aps]
        for k, value in enumerate(values):
            for n in range(KP):
                for m in range(KP):
                    slot = tgt[i * (KP * KA * KP) + n * (KA * KP) + k * KP + m]
                    acc[slot] += value[n * B:(n + 1) * B, m * LANES:(m + 1) * LANES]


def products(a_rows, columns, p_rows, chosen, slots):
    vmem = pl.BlockSpec(memory_space=pltpu.VMEM)
    smem = pl.BlockSpec(memory_space=pltpu.SMEM)
    return pl.pallas_call(
        product_kernel,
        out_shape=pltpu.VMEM((SLOTS, B, LANES), f32),
        in_specs=[smem, smem, pl.BlockSpec(memory_space=pl.ANY), vmem, vmem],
        out_specs=vmem,
        scratch_shapes=[
            pltpu.VMEM((A_SLOTS, KA, B, B), bf16),
            pltpu.VMEM((KP * B, B), bf16),
            pltpu.SemaphoreType.DMA((A_SLOTS,))],
        compiler_params=pltpu.CompilerParams(vmem_limit_bytes=8 << 20),
        name="products",
    )(columns.reshape(-1), slots.reshape(-1), a_rows, p_rows, chosen)


def wire(step):
    return f32 if step >= WIDE_FROM else bf16


def scatter_kernel(acc, out_ref, *refs):
    refs = list(refs)
    cross, other = refs.pop(0), refs.pop(0)
    keep = [refs.pop(0) for _ in range(STEPS)]
    give = [refs.pop(0) for _ in range(STEPS)]
    got = [refs.pop(0) for _ in range(STEPS)]
    core_send, core_recv, send_sem, recv_sem = refs
    grp, blk = lax.axis_index("grp"), lax.axis_index("blk")
    bits = bits_of(grp, blk)
    partners = {bit: partner_of(grp, blk, bit) for bit in BITS + ("core",)}
    core = bits["core"]
    lane = lax.broadcasted_iota(jnp.int32, (24, LANES), 1)

    def packed(part, side, entry):
        owner = side * 64 + entry % (1 << part) * (1 << (STEPS - part)) + entry // (1 << part)
        units = []
        for unit in (2 * (part % 3), 2 * (part % 3) + 1):
            j, u = part // 3 * 2 + unit // 3, unit % 3
            main = acc[owner * OWN + j, 24 * u:24 * u + 24]
            tail = acc[owner * OWN + j, PACK:]
            units.append(jnp.where(lane < B, main, pltpu.roll(tail, 96 - 32 * u, 1)))
        return jnp.concatenate(units, axis=0)

    enter(list(partners.values()))
    crossed = []
    for part in range(PARTS):
        def pack(e, _):
            cross[part, e] = packed(part, 1 - core, e).astype(bf16)
            return 0
        lax.fori_loop(0, 64, pack, 0, unroll=4)
        copy = pltpu.make_async_remote_copy(
            src_ref=cross.at[part], dst_ref=other.at[part],
            send_sem=core_send.at[part], recv_sem=core_recv.at[part],
            device_id=partners["core"], device_id_type=MESH)
        copy.start()
        crossed.append(copy)
    sends = [[None] * PARTS for _ in range(STEPS)]
    for step in range(STEPS):
        half = 32 >> step
        for part in range(PARTS):
            bit = order_of(part)[step]
            away, here = (1 - bits[bit]) * half, bits[bit] * half
            if step == 0:
                crossed[part].wait_recv()
            else:
                sends[step - 1][part].wait_recv()

            def combine(offset, target, dtype):
                def one(e, _):
                    if step == 0:
                        total = packed(part, core, offset + e) + other[part, offset + e].astype(f32)
                    else:
                        total = keep[step - 1][part, offset + e] + got[step - 1][part, offset + e].astype(f32)
                    target[part, e] = total.astype(dtype)
                    return 0
                lax.fori_loop(0, half, one, 0, unroll=min(half, 4))

            combine(away, give[step], wire(step))
            copy = pltpu.make_async_remote_copy(
                src_ref=give[step].at[part], dst_ref=got[step].at[part],
                send_sem=send_sem.at[step, part], recv_sem=recv_sem.at[step, part],
                device_id=partners[bit], device_id_type=MESH)
            copy.start()
            sends[step][part] = copy
            combine(here, keep[step], f32)
    pieces = []
    for part in range(PARTS):
        sends[-1][part].wait_recv()
        pieces.append(keep[-1][part, 0] + got[-1][part, 0])
    for pair in range(2):
        both = jnp.concatenate(pieces[pair * 3:pair * 3 + 3], axis=0)
        for j in range(2):
            block = both[j * PACK:(j + 1) * PACK]
            out_ref[0, pair * 2 + j, :PACK] = block[:, :B]
            out_ref[0, pair * 2 + j, PACK:] = unfold(block)[:, :B]
    for copy in crossed:
        copy.wait_send()
    for row in sends:
        for copy in row:
            copy.wait_send()


def scatter(acc):
    halves = [32 >> step for step in range(STEPS)]
    return pl.pallas_call(
        scatter_kernel,
        out_shape=jax.ShapeDtypeStruct((1, OWN, B, B), f32),
        in_specs=[pl.BlockSpec(memory_space=pltpu.VMEM)],
        out_specs=pl.BlockSpec(memory_space=pltpu.VMEM),
        scratch_shapes=(
            [pltpu.VMEM((PARTS, 64, PIECE, LANES), bf16)] * 2
            + [pltpu.VMEM((PARTS, n, PIECE, LANES), f32) for n in halves]
            + [pltpu.VMEM((PARTS, n, PIECE, LANES), wire(s)) for s, n in enumerate(halves)] * 2
            + [pltpu.SemaphoreType.DMA((PARTS,))] * 2
            + [pltpu.SemaphoreType.DMA((STEPS, PARTS))] * 2),
        compiler_params=pltpu.CompilerParams(collective_id=1, has_side_effects=True, vmem_limit_bytes=34 << 20),
        name="sum_at_owners",
    )(pltpu.with_memory_space_constraint(acc, pltpu.VMEM))


def shards(a_blocks, col_index, prolong, target):
    chosen = gather(prolong[0])
    acc = products(a_blocks[0], col_index[0], prolong[0], chosen, slot_of(target[0]))
    return scatter(acc)


def solution(mesh):
    return jax.shard_map(
        shards,
        mesh=mesh,
        in_specs=(
            P("grp", "blk", None, None, None),
            P("grp", "blk", None),
            P("grp", "blk", None, None, None),
            P("grp", "blk", None),
        ),
        out_specs=P("grp", "blk", None, None),
        check_vma=False,
    )
```

time: 216 us -> 152 us (0.70)
  Pallas kernels: 208 us -> 147 us
  local copies, waits for them, and re-layouts: 7.55 us -> 4.47 us
    pallas_call x2, Pallas kernels: 162 us -> 89.4 us  [the longest x1 50.5 us: gather(): pl.pallas_call(gather_kernel, out_shape=jax.ShapeDtypeStruct((FR * MEMBER...]
    pallas_call x1, Pallas kernels: 45.6 us -> 57.4 us  [scatter(): pl.pallas_call(scatter_kernel, out_shape=jax.ShapeDtypeStruct((1, OWN, B,...]
    unnamed x5 -> x3, local copies, waits for them, and re-layouts: 4.77 us -> 2.88 us
where the time goes in v2:
time: 152 us; the launch traced here: 151 us
  Pallas kernels  147 us (97%)
  local copies, waits for them, and re-layouts  4.47 us (3%)
    pallas_call x1, Pallas kernels, scatter(): pl.pallas_call(scatter_kernel, out_shape=jax.ShapeDtypeStruct((1, OWN, B,...  57.4 us
    pallas_call x1, Pallas kernels, gather(): pl.pallas_call(gather_kernel, out_shape=jax.ShapeDtypeStruct((FR * MEMBER...  50.5 us
    pallas_call x1, Pallas kernels, products(): pl.pallas_call(product_kernel, out_shape=pltpu.VMEM((SLOTS, B, LANES), f3...  38.9 us

profile of v2, /device:TPU:0, one launch (start us, length us, event | category | flops | bytes accessed | tf_op | source)
XLA Modules:
  0.0 151.4 jit_solution(5111717097478571754)
XLA Ops:
  0.0 0.8 reshape_squeeze.3.col
  0.8 0.8 squeeze.10
  1.6 0.1 fusion.13.tgt
  1.7 0.0 copy-start
  1.7 1.3 copy-done
  3.0 50.5 %gather_prolong.1.chosen = bf16[192,96,256]{2,1,0:T(8,128)(2,1)S(1)} custom-call(bf16[24,2,96,96]{3,2,1,0:T(8,128)(2,1)S(1)} %bitcast.2), custom_call_target="tpu_custom_call" | custom-call | tf_op jit(solution)/shard_map/gather_prolong/pallas_call | solution.py:169
  53.5 38.9 %products.1.acc = f32[512,96,128]{2,1,0:T(8,128)S(1)} custom-call(s32[648]{0:T(1024)S(1)} %reshape_squeeze.3.col, s32[2592]{0:T(1024)S(1)} %fusion.13.tgt, bf16[24,27,96,96]{3,2,1,0:T(8,128)(2,1)} %bitcast.4, bf16[24,2,96,96]{3,2,1,0:T(8,128)(2,1)S(1)} %bitcast.3, bf16[192,96,256]{2,1,0:T(8,128)(2,1)S(1)} %gather_prolong.1.chosen), custom_call_target="tpu_custom_call" | custom-call | tf_op jit(solution)/shard_map/products/pallas_call | solution.py:222
  92.4 57.4 %sum_at_owners.1 = f32[1,4,96,96]{3,2,1,0:T(8,128)} custom-call(f32[512,96,128]{2,1,0:T(8,128)S(1)} %products.1.acc), custom_call_target="tpu_custom_call" | custom-call | tf_op jit(solution)/shard_map/sum_at_owners/pallas_call | solution.py:324
  149.8 1.6 %copy.6 = f32[1,4,96,96]{3,2,1,0:T(8,128)} copy(f32[1,4,96,96]{3,2,1,0:T(8,128)} %sum_at_owners.1) | data formatting | bytes 294912
Async XLA Ops:
  1.7 1.3 copy-start

commit v3 on v2

--- a/solution.py
+++ b/solution.py
@@ -23,7 +23,6 @@
 PARTS = 6
 PIECE = OWN * PACK // PARTS
 STEPS = 6
-WIDE_FROM = 2
 
 BITS = ("xg", "yg", "zg", "xh", "yh", "zh")
 
@@ -180,6 +179,7 @@
 
 
 A_SLOTS = 3
+AHEAD = 8
 
 
 def product_kernel(col, tgt, a_ref, p_ref, chosen, acc, a_buf, p_trans, a_sem):
@@ -207,9 +207,16 @@
             fetch(i + A_SLOTS - 1).start()
 
         a = a_buf.at[i % A_SLOTS]
-        aps = [jnp.dot(a[k], chosen[col[i * KA + k]], preferred_element_type=f32).astype(bf16) for k in range(KA)]
-        values = [jnp.dot(pt, ap, preferred_element_type=f32) for ap in aps]
-        for k, value in enumerate(values):
+        aps, values = {}, {}
+        for u in range(KA + 2 * AHEAD):
+            if u < KA:
+                aps[u] = jnp.dot(a[u], chosen[col[i * KA + u]], preferred_element_type=f32).astype(bf16)
+            if 0 <= u - AHEAD < KA:
+                values[u - AHEAD] = jnp.dot(pt, aps.pop(u - AHEAD), preferred_element_type=f32)
+            k = u - 2 * AHEAD
+            if k < 0:
+                continue
+            value = values.pop(k)
             for n in range(KP):
                 for m in range(KP):
                     slot = tgt[i * (KP * KA * KP) + n * (KA * KP) + k * KP + m]
@@ -233,22 +240,26 @@
     )(columns.reshape(-1), slots.reshape(-1), a_rows, p_rows, chosen)
 
 
-def wire(step):
-    return f32 if step >= WIDE_FROM else bf16
-
-
-def scatter_kernel(acc, out_ref, *refs):
-    refs = list(refs)
-    cross, other = refs.pop(0), refs.pop(0)
-    keep = [refs.pop(0) for _ in range(STEPS)]
-    give = [refs.pop(0) for _ in range(STEPS)]
-    got = [refs.pop(0) for _ in range(STEPS)]
-    core_send, core_recv, send_sem, recv_sem = refs
+def flipped(grp, blk, flips):
+    place = {"grp": grp, "blk": blk}
+    for bit in flips:
+        place = partner_of(place["grp"], place["blk"], bit)
+    return place
+
+
+def direct(part, relative):
+    return [bit for i, bit in enumerate(order_of(part)[3:]) if relative >> (2 - i) & 1]
+
+
+def scatter_kernel(acc, out_ref, cross, other, keep0, give0, got0, keep1, give1, got1, keep2, give2, got2, last, arrived, total,
+                   core_send, core_recv, send0, recv0, send1, recv1, send2, recv2, last_send, last_recv):
     grp, blk = lax.axis_index("grp"), lax.axis_index("blk")
     bits = bits_of(grp, blk)
-    partners = {bit: partner_of(grp, blk, bit) for bit in BITS + ("core",)}
     core = bits["core"]
+    mine = [[bits[bit] for bit in order_of(part)] for part in range(PARTS)]
     lane = lax.broadcasted_iota(jnp.int32, (24, LANES), 1)
+    flips = sorted({tuple(sorted(direct(part, r))) for part in range(PARTS) for r in range(1, 8)}) + [("core",)]
+    partners = {f: flipped(grp, blk, f) for f in flips}
 
     def packed(part, side, entry):
         owner = side * 64 + entry % (1 << part) * (1 << (STEPS - part)) + entry // (1 << part)
@@ -260,79 +271,129 @@
             units.append(jnp.where(lane < B, main, pltpu.roll(tail, 96 - 32 * u, 1)))
         return jnp.concatenate(units, axis=0)
 
-    enter(list(partners.values()))
-    crossed = []
-    for part in range(PARTS):
-        def pack(e, _):
-            cross[part, e] = packed(part, 1 - core, e).astype(bf16)
+    def fill(target, n, value):
+        def one(e, _):
+            target[e] = value(e).astype(target.dtype)
             return 0
-        lax.fori_loop(0, 64, pack, 0, unroll=4)
+        lax.fori_loop(0, n, one, 0, unroll=4)
+
+    started = []
+
+    def send(source, target, send_sem, recv_sem, device):
         copy = pltpu.make_async_remote_copy(
-            src_ref=cross.at[part], dst_ref=other.at[part],
-            send_sem=core_send.at[part], recv_sem=core_recv.at[part],
-            device_id=partners["core"], device_id_type=MESH)
+            src_ref=source, dst_ref=target, send_sem=send_sem, recv_sem=recv_sem,
+            device_id=device, device_id_type=MESH)
         copy.start()
-        crossed.append(copy)
-    sends = [[None] * PARTS for _ in range(STEPS)]
-    for step in range(STEPS):
-        half = 32 >> step
+        started.append(copy)
+        return copy
+
+    barrier = pltpu.get_barrier_semaphore()
+    for device in partners.values():
+        pl.semaphore_signal(barrier, inc=1, device_id=device, device_id_type=MESH)
+
+    crossed, first, second, third, final = {}, {}, {}, {}, {}
+    for chunk in range(2):
         for part in range(PARTS):
-            bit = order_of(part)[step]
-            away, here = (1 - bits[bit]) * half, bits[bit] * half
-            if step == 0:
-                crossed[part].wait_recv()
-            else:
-                sends[step - 1][part].wait_recv()
-
-            def combine(offset, target, dtype):
-                def one(e, _):
-                    if step == 0:
-                        total = packed(part, core, offset + e) + other[part, offset + e].astype(f32)
-                    else:
-                        total = keep[step - 1][part, offset + e] + got[step - 1][part, offset + e].astype(f32)
-                    target[part, e] = total.astype(dtype)
-                    return 0
-                lax.fori_loop(0, half, one, 0, unroll=min(half, 4))
-
-            combine(away, give[step], wire(step))
-            copy = pltpu.make_async_remote_copy(
-                src_ref=give[step].at[part], dst_ref=got[step].at[part],
-                send_sem=send_sem.at[step, part], recv_sem=recv_sem.at[step, part],
-                device_id=partners[bit], device_id_type=MESH)
-            copy.start()
-            sends[step][part] = copy
-            combine(here, keep[step], f32)
+            offset = (1 - mine[part][0] if chunk == 0 else mine[part][0]) * 32
+            fill(cross.at[part, chunk], 32, lambda e: packed(part, 1 - core, offset + e))
+            if chunk == 0 and part == 0:
+                pl.semaphore_wait(barrier, len(flips))
+            crossed[part, chunk] = send(
+                cross.at[part, chunk], other.at[part, chunk], core_send.at[part, chunk], core_recv.at[part, chunk],
+                partners[("core",)])
+
+    for part in range(PARTS):
+        crossed[part, 0].wait_recv()
+        for chunk in range(2):
+            offset = (1 - mine[part][1] if chunk == 0 else mine[part][1]) * 16
+            away = (1 - mine[part][0]) * 32 + offset
+            fill(give0.at[part, chunk], 16,
+                 lambda e: packed(part, core, away + e) + other[part, 0, offset + e].astype(f32))
+            first[part, chunk] = send(
+                give0.at[part, chunk], got0.at[part, chunk], send0.at[part, chunk], recv0.at[part, chunk],
+                partners[(order_of(part)[0],)])
+    for part in range(PARTS):
+        crossed[part, 1].wait_recv()
+        for chunk in range(2):
+            offset = (1 - mine[part][1] if chunk == 0 else mine[part][1]) * 16
+            here = mine[part][0] * 32 + offset
+            fill(keep0.at[part, chunk], 16,
+                 lambda e: packed(part, core, here + e) + other[part, 1, offset + e].astype(f32))
+
+    for part in range(PARTS):
+        first[part, 0].wait_recv()
+        for chunk in range(2):
+            offset = (1 - mine[part][2] if chunk == 0 else mine[part][2]) * 8
+            fill(give1.at[part, chunk], 8,
+                 lambda e: keep0[part, 0, offset + e] + got0[part, 0, offset + e].astype(f32))
+            second[part, chunk] = send(
+                give1.at[part, chunk], got1.at[part, chunk], send1.at[part, chunk], recv1.at[part, chunk],
+                partners[(order_of(part)[1],)])
+    for part in range(PARTS):
+        first[part, 1].wait_recv()
+        for chunk in range(2):
+            offset = (1 - mine[part][2] if chunk == 0 else mine[part][2]) * 8
+            fill(keep1.at[part, chunk], 8,
+                 lambda e: keep0[part, 1, offset + e] + got0[part, 1, offset + e].astype(f32))
+
+    for part in range(PARTS):
+        second[part, 0].wait_recv()
+        fill(give2.at[part], 8, lambda e: keep1[part, 0, e] + got1[part, 0, e].astype(f32))
+        third[part] = send(
+            give2.at[part], got2.at[part], send2.at[part], recv2.at[part], partners[(order_of(part)[2],)])
+    for part in range(PARTS):
+        second[part, 1].wait_recv()
+        fill(keep2.at[part], 8, lambda e: keep1[part, 1, e] + got1[part, 1, e].astype(f32))
+
+    for part in range(PARTS):
+        third[part].wait_recv()
+        for r in range(8):
+            entry = 0
+            for i in range(3):
+                bit = mine[part][3 + i]
+                entry = entry * 2 + (1 - bit if r >> (2 - i) & 1 else bit)
+            value = keep2[part, entry] + got2[part, entry].astype(f32)
+            if r == 0:
+                total[part] = value
+                continue
+            last[part, r - 1] = value.astype(bf16)
+            final[part, r] = send(
+                last.at[part, r - 1], arrived.at[part, r - 1], last_send.at[part, r - 1], last_recv.at[part, r - 1],
+                partners[tuple(sorted(direct(part, r)))])
     pieces = []
     for part in range(PARTS):
-        sends[-1][part].wait_recv()
-        pieces.append(keep[-1][part, 0] + got[-1][part, 0])
+        value = total[part]
+        for r in range(1, 8):
+            final[part, r].wait_recv()
+            value = value + arrived[part, r - 1].astype(f32)
+        pieces.append(value)
     for pair in range(2):
         both = jnp.concatenate(pieces[pair * 3:pair * 3 + 3], axis=0)
         for j in range(2):
             block = both[j * PACK:(j + 1) * PACK]
             out_ref[0, pair * 2 + j, :PACK] = block[:, :B]
             out_ref[0, pair * 2 + j, PACK:] = unfold(block)[:, :B]
-    for copy in crossed:
+    for copy in started:
         copy.wait_send()
-    for row in sends:
-        for copy in row:
-            copy.wait_send()
 
 
 def scatter(acc):
-    halves = [32 >> step for step in range(STEPS)]
+    def piece(dtype, *lead):
+        return pltpu.VMEM((PARTS,) + lead + (PIECE, LANES), dtype)
+    dma = pltpu.SemaphoreType.DMA
     return pl.pallas_call(
         scatter_kernel,
         out_shape=jax.ShapeDtypeStruct((1, OWN, B, B), f32),
         in_specs=[pl.BlockSpec(memory_space=pltpu.VMEM)],
         out_specs=pl.BlockSpec(memory_space=pltpu.VMEM),
-        scratch_shapes=(
-            [pltpu.VMEM((PARTS, 64, PIECE, LANES), bf16)] * 2
-            + [pltpu.VMEM((PARTS, n, PIECE, LANES), f32) for n in halves]
-            + [pltpu.VMEM((PARTS, n, PIECE, LANES), wire(s)) for s, n in enumerate(halves)] * 2
-            + [pltpu.SemaphoreType.DMA((PARTS,))] * 2
-            + [pltpu.SemaphoreType.DMA((STEPS, PARTS))] * 2),
-        compiler_params=pltpu.CompilerParams(collective_id=1, has_side_effects=True, vmem_limit_bytes=34 << 20),
+        scratch_shapes=[
+            piece(bf16, 2, 32), piece(bf16, 2, 32),
+            piece(f32, 2, 16), piece(bf16, 2, 16), piece(bf16, 2, 16),
+            piece(f32, 2, 8), piece(bf16, 2, 8), piece(bf16, 2, 8),
+            piece(f32, 8), piece(bf16, 8), piece(bf16, 8),
+            piece(bf16, 7), piece(bf16, 7), piece(f32)]
+            + [dma((PARTS, 2))] * 6 + [dma((PARTS,))] * 2 + [dma((PARTS, 7))] * 2,
+        compiler_params=pltpu.CompilerParams(collective_id=1, has_side_effects=True, vmem_limit_bytes=30 << 20),
         name="sum_at_owners",
     )(pltpu.with_memory_space_constraint(acc, pltpu.VMEM))
 

time: 152 us -> 137 us (0.901)
  Pallas kernels: 147 us -> 132 us
    pallas_call x1, Pallas kernels: 57.4 us -> 44.7 us  [scatter(): pl.pallas_call(scatter_kernel, out_shape=jax.ShapeDtypeStruct((1, OWN, B,...]
    pallas_call x1, Pallas kernels: 38.9 us -> 36.6 us  [products(): pl.pallas_call(product_kernel, out_shape=pltpu.VMEM((SLOTS, B, LANES), f3...]
where the time goes in v3:
time: 137 us; the launch traced here: 136 us
  Pallas kernels  132 us (96%)
  local copies, waits for them, and re-layouts  4.47 us (3%)
    pallas_call x1, Pallas kernels, gather(): pl.pallas_call(gather_kernel, out_shape=jax.ShapeDtypeStruct((FR * MEMBER...  50.5 us
    pallas_call x1, Pallas kernels, scatter(): pl.pallas_call(scatter_kernel, out_shape=jax.ShapeDtypeStruct((1, OWN, B,...  44.7 us
    pallas_call x1, Pallas kernels, products(): pl.pallas_call(product_kernel, out_shape=pltpu.VMEM((SLOTS, B, LANES), f3...  36.6 us
    unnamed x3, local copies, waits for them, and re-layouts  2.88 us

profile of v3, /device:TPU:0, one launch (start us, length us, event | category | flops | bytes accessed | tf_op | source)
XLA Modules:
  0.0 136.5 jit_solution(971173343506161456)
XLA Ops:
  0.0 0.8 reshape_squeeze.3.col
  0.8 0.8 squeeze.10
  1.6 0.1 fusion.13.tgt
  1.7 0.0 copy-start
  1.7 1.3 copy-done
  3.0 50.5 %gather_prolong.1.chosen = bf16[192,96,256]{2,1,0:T(8,128)(2,1)S(1)} custom-call(bf16[24,2,96,96]{3,2,1,0:T(8,128)(2,1)S(1)} %bitcast.2), custom_call_target="tpu_custom_call" | custom-call | tf_op jit(solution)/shard_map/gather_prolong/pallas_call | solution.py:168
  53.5 36.6 %products.1.acc = f32[512,96,128]{2,1,0:T(8,128)S(1)} custom-call(s32[648]{0:T(1024)S(1)} %reshape_squeeze.3.col, s32[2592]{0:T(1024)S(1)} %fusion.13.tgt, bf16[24,27,96,96]{3,2,1,0:T(8,128)(2,1)} %bitcast.4, bf16[24,2,96,96]{3,2,1,0:T(8,128)(2,1)S(1)} %bitcast.3, bf16[192,96,256]{2,1,0:T(8,128)(2,1)S(1)} %gather_prolong.1.chosen), custom_call_target="tpu_custom_call" | custom-call | tf_op jit(solution)/shard_map/products/pallas_call | solution.py:229
  90.2 44.7 %sum_at_owners.1 = f32[1,4,96,96]{3,2,1,0:T(8,128)} custom-call(f32[512,96,128]{2,1,0:T(8,128)S(1)} %products.1.acc), custom_call_target="tpu_custom_call" | custom-call | tf_op jit(solution)/shard_map/sum_at_owners/pallas_call | solution.py:384
  134.9 1.6 %copy.6 = f32[1,4,96,96]{3,2,1,0:T(8,128)} copy(f32[1,4,96,96]{3,2,1,0:T(8,128)} %sum_at_owners.1) | data formatting | bytes 294912
Async XLA Ops:
  1.7 1.3 copy-start

commit v4 on v3

--- a/solution.py
+++ b/solution.py
@@ -70,13 +70,6 @@
     return index * OWN + target % OWN
 
 
-def enter(partners):
-    barrier = pltpu.get_barrier_semaphore()
-    for device in partners:
-        pl.semaphore_signal(barrier, inc=1, device_id=device, device_id_type=MESH)
-    pl.semaphore_wait(barrier, len(partners))
-
-
 def fold(main, tail):
     lane = lax.broadcasted_iota(jnp.int32, main.shape, 1)
     side = jnp.concatenate([pltpu.roll(tail, shift, 1) for shift in (96, 64, 32)], axis=0)
@@ -95,6 +88,7 @@
 G_ORDERS = (("xg", "xh", "zl"), ("xh", "zl", "xg"), ("zl", "xg", "xh"))
 G_PARTS = 3
 G_ROWS = FR // G_PARTS
+G_BATCH = 4
 
 
 def member(part, blk, flip):
@@ -112,17 +106,22 @@
 def gather_kernel(p_ref, out_ref, landed, send_sem, recv_sem):
     grp, blk = lax.axis_index("grp"), lax.axis_index("blk")
     partners = {bit: partner_of(grp, blk, bit) for bit in G_ORDERS[0]}
+    barrier = pltpu.get_barrier_semaphore()
+    for device in partners.values():
+        pl.semaphore_signal(barrier, inc=1, device_id=device, device_id_type=MESH)
     where = [[member(part, blk, flip) for flip in range(MEMBERS)] for part in range(G_PARTS)]
     for part in range(G_PARTS):
         mine = where[part][0][0]
 
-        def pack(r, _):
-            v = p_ref[part * G_ROWS + r].astype(f32)
-            v = jnp.pad(v.reshape(KP * B, B), ((0, 0), (0, LANES - B)))
-            landed[part, mine, r] = fold(v[:KP * PACK], v[KP * PACK:]).astype(bf16)
-            return 0
-        lax.fori_loop(0, G_ROWS, pack, 0, unroll=True)
-    enter(list(partners.values()))
+        for low in range(0, G_ROWS, G_BATCH):
+            packed = []
+            for r in range(low, low + G_BATCH):
+                v = p_ref[part * G_ROWS + r].reshape(KP * B, B)
+                v = jnp.pad(v, ((0, 0), (0, LANES - B)))
+                packed.append(fold(v[:KP * PACK], v[KP * PACK:]))
+            for r in range(G_BATCH):
+                landed[part, mine, low + r] = packed[r]
+    pl.semaphore_wait(barrier, len(partners))
     sends = []
     arrivals = {}
 
@@ -139,14 +138,14 @@
     def unpack(part, flip):
         index, source = where[part][flip]
 
-        def one(r, _):
-            packed = landed[part, index, r]
-            both = jnp.concatenate([packed, unfold(packed)], axis=0)
-            row = source * FR + part * G_ROWS + r
-            for n in range(KP):
-                out_ref[row, :, n * LANES:(n + 1) * LANES] = both[n * B:(n + 1) * B]
-            return 0
-        lax.fori_loop(0, G_ROWS, one, 0, unroll=True)
+        row = source * FR + part * G_ROWS
+        for low in range(0, G_ROWS, G_BATCH):
+            packed = [landed[part, index, low + r] for r in range(G_BATCH)]
+            tails = [unfold(v) for v in packed]
+            for r in range(G_BATCH):
+                both = jnp.concatenate([packed[r], tails[r]], axis=0)
+                for n in range(KP):
+                    out_ref[row + low + r, :, n * LANES:(n + 1) * LANES] = both[n * B:(n + 1) * B]
 
     for step in range(3):
         for part in range(G_PARTS):
@@ -240,6 +239,9 @@
     )(columns.reshape(-1), slots.reshape(-1), a_rows, p_rows, chosen)
 
 
+BATCH = 16
+
+
 def flipped(grp, blk, flips):
     place = {"grp": grp, "blk": blk}
     for bit in flips:
@@ -272,10 +274,13 @@
         return jnp.concatenate(units, axis=0)
 
     def fill(target, n, value):
-        def one(e, _):
-            target[e] = value(e).astype(target.dtype)
+        def some(g, _):
+            values = [value(g * batch + e).astype(target.dtype) for e in range(batch)]
+            for e in range(batch):
+                target[g * batch + e] = values[e]
             return 0
-        lax.fori_loop(0, n, one, 0, unroll=4)
+        batch = min(n, BATCH)
+        lax.fori_loop(0, n // batch, some, 0)
 
     started = []
 
@@ -292,17 +297,16 @@
         pl.semaphore_signal(barrier, inc=1, device_id=device, device_id_type=MESH)
 
     crossed, first, second, third, final = {}, {}, {}, {}, {}
-    for chunk in range(2):
-        for part in range(PARTS):
-            offset = (1 - mine[part][0] if chunk == 0 else mine[part][0]) * 32
-            fill(cross.at[part, chunk], 32, lambda e: packed(part, 1 - core, offset + e))
-            if chunk == 0 and part == 0:
-                pl.semaphore_wait(barrier, len(flips))
-            crossed[part, chunk] = send(
-                cross.at[part, chunk], other.at[part, chunk], core_send.at[part, chunk], core_recv.at[part, chunk],
-                partners[("core",)])
-
-    for part in range(PARTS):
+    def cross_over(part, chunk):
+        offset = (1 - mine[part][0] if chunk == 0 else mine[part][0]) * 32
+        fill(cross.at[part, chunk], 32, lambda e: packed(part, 1 - core, offset + e))
+        if chunk == 0 and part == 0:
+            pl.semaphore_wait(barrier, len(flips))
+        crossed[part, chunk] = send(
+            cross.at[part, chunk], other.at[part, chunk], core_send.at[part, chunk], core_recv.at[part, chunk],
+            partners[("core",)])
+
+    def give_away(part):
         crossed[part, 0].wait_recv()
         for chunk in range(2):
             offset = (1 - mine[part][1] if chunk == 0 else mine[part][1]) * 16
@@ -312,6 +316,15 @@
             first[part, chunk] = send(
                 give0.at[part, chunk], got0.at[part, chunk], send0.at[part, chunk], recv0.at[part, chunk],
                 partners[(order_of(part)[0],)])
+
+    cross_over(0, 0)
+    cross_over(1, 0)
+    for part in range(PARTS):
+        if part + 2 < PARTS:
+            cross_over(part + 2, 0)
+        give_away(part)
+    for part in range(PARTS):
+        cross_over(part, 1)
     for part in range(PARTS):
         crossed[part, 1].wait_recv()
         for chunk in range(2):

time: 137 us -> 129 us (0.942)
  Pallas kernels: 132 us -> 124 us
    pallas_call x1, Pallas kernels: 44.7 us -> 37 us  [scatter(): pl.pallas_call(scatter_kernel, out_shape=jax.ShapeDtypeStruct((1, OWN, B,...]
where the time goes in v4:
time: 129 us
  Pallas kernels  124 us (96%)
  local copies, waits for them, and re-layouts  4.47 us (3%)
    pallas_call x1, Pallas kernels, gather(): pl.pallas_call(gather_kernel, out_shape=jax.ShapeDtypeStruct((FR * MEMBER...  50.2 us
    pallas_call x1, Pallas kernels, scatter(): pl.pallas_call(scatter_kernel, out_shape=jax.ShapeDtypeStruct((1, OWN, B,...  37 us
    pallas_call x1, Pallas kernels, products(): pl.pallas_call(product_kernel, out_shape=pltpu.VMEM((SLOTS, B, LANES), f3...  36.8 us
    unnamed x3, local copies, waits for them, and re-layouts  2.88 us

profile of v4, /device:TPU:0, one launch (start us, length us, event | category | flops | bytes accessed | tf_op | source)
XLA Modules:
  0.0 128.7 jit_solution(11049205737331973564)
XLA Ops:
  0.0 0.8 reshape_squeeze.3.col
  0.8 0.8 squeeze.10
  1.6 0.1 fusion.13.tgt
  1.7 0.0 copy-start
  1.7 1.3 copy-done
  3.0 50.2 %gather_prolong.1.chosen = bf16[192,96,256]{2,1,0:T(8,128)(2,1)S(1)} custom-call(bf16[24,2,96,96]{3,2,1,0:T(8,128)(2,1)S(1)} %bitcast.2), custom_call_target="tpu_custom_call" | custom-call | tf_op jit(solution)/shard_map/gather_prolong/pallas_call | solution.py:167
  53.2 36.8 %products.1.acc = f32[512,96,128]{2,1,0:T(8,128)S(1)} custom-call(s32[648]{0:T(1024)S(1)} %reshape_squeeze.3.col, s32[2592]{0:T(1024)S(1)} %fusion.13.tgt, bf16[24,27,96,96]{3,2,1,0:T(8,128)(2,1)} %bitcast.4, bf16[24,2,96,96]{3,2,1,0:T(8,128)(2,1)S(1)} %bitcast.3, bf16[192,96,256]{2,1,0:T(8,128)(2,1)S(1)} %gather_prolong.1.chosen), custom_call_target="tpu_custom_call" | custom-call | tf_op jit(solution)/shard_map/products/pallas_call | solution.py:228
  90.0 37.0 %sum_at_owners.1 = f32[1,4,96,96]{3,2,1,0:T(8,128)} custom-call(f32[512,96,128]{2,1,0:T(8,128)S(1)} %products.1.acc), custom_call_target="tpu_custom_call" | custom-call | tf_op jit(solution)/shard_map/sum_at_owners/pallas_call | solution.py:397
  127.0 1.6 %copy.6 = f32[1,4,96,96]{3,2,1,0:T(8,128)} copy(f32[1,4,96,96]{3,2,1,0:T(8,128)} %sum_at_owners.1) | data formatting | bytes 294912
Async XLA Ops:
  1.7 1.3 copy-start

commit v5 on v4

--- a/solution.py
+++ b/solution.py
@@ -103,7 +103,13 @@
     return index, bits["zl"] * 4 + bits["xh"] * 2 + (bits["xh"] + bits["xg"]) % 2
 
 
-def gather_kernel(p_ref, out_ref, landed, send_sem, recv_sem):
+def gather_kernel(p_hbm, out_ref, trans_ref, p_ref, landed, load_sem, send_sem, recv_sem):
+    loads = []
+    for part in range(G_PARTS):
+        rows = pl.ds(part * G_ROWS, G_ROWS)
+        load = pltpu.make_async_copy(p_hbm.at[rows], p_ref.at[rows], load_sem.at[part])
+        load.start()
+        loads.append(load)
     grp, blk = lax.axis_index("grp"), lax.axis_index("blk")
     partners = {bit: partner_of(grp, blk, bit) for bit in G_ORDERS[0]}
     barrier = pltpu.get_barrier_semaphore()
@@ -112,6 +118,7 @@
     where = [[member(part, blk, flip) for flip in range(MEMBERS)] for part in range(G_PARTS)]
     for part in range(G_PARTS):
         mine = where[part][0][0]
+        loads[part].wait()
 
         for low in range(0, G_ROWS, G_BATCH):
             packed = []
@@ -152,6 +159,11 @@
             forward(part, 0, step)
     for part in range(G_PARTS):
         unpack(part, 0)
+
+    @pl.loop(0, FR)
+    def _(r):
+        for n in range(KP):
+            trans_ref[r, n * B:(n + 1) * B, :] = p_ref[r, n].T
     for flip in range(1, MEMBERS):
         for part in range(G_PARTS):
             arrivals[part, flip].wait_recv()
@@ -166,27 +178,32 @@
 def gather(prolong):
     return pl.pallas_call(
         gather_kernel,
-        out_shape=jax.ShapeDtypeStruct((FR * MEMBERS, B, KP * LANES), bf16),
-        in_specs=[pl.BlockSpec(memory_space=pltpu.VMEM)],
-        out_specs=pl.BlockSpec(memory_space=pltpu.VMEM),
+        out_shape=(
+            jax.ShapeDtypeStruct((FR * MEMBERS, B, KP * LANES), bf16),
+            jax.ShapeDtypeStruct((FR, KP * B, B), bf16)),
+        in_specs=[pl.BlockSpec(memory_space=pl.ANY)],
+        out_specs=(pl.BlockSpec(memory_space=pltpu.VMEM), pl.BlockSpec(memory_space=pltpu.VMEM)),
         scratch_shapes=[
+            pltpu.VMEM((FR, KP, B, B), bf16),
             pltpu.VMEM((G_PARTS, MEMBERS, G_ROWS, KP * PACK, LANES), bf16),
+            pltpu.SemaphoreType.DMA((G_PARTS,)),
             pltpu.SemaphoreType.DMA((G_PARTS, MEMBERS)), pltpu.SemaphoreType.DMA((G_PARTS, MEMBERS))],
         compiler_params=pltpu.CompilerParams(collective_id=0, has_side_effects=True, vmem_limit_bytes=20 << 20),
         name="gather_prolong",
-    )(prolong)
-
-
-A_SLOTS = 3
-AHEAD = 8
-
-
-def product_kernel(col, tgt, a_ref, p_ref, chosen, acc, a_buf, p_trans, a_sem):
+    )(pltpu.with_memory_space_constraint(prolong, pltpu.HBM))
+
+
+ROWS = 4
+A_SLOTS = 8
+AHEAD = 4
+
+
+def product_kernel(col, tgt, a_ref, p_trans, chosen, acc, a_buf, a_sem):
     def fetch(i):
         slot = i % A_SLOTS
         return pltpu.make_async_copy(a_ref.at[i], a_buf.at[slot], a_sem.at[slot])
 
-    for i in range(A_SLOTS - 1):
+    for i in range(A_SLOTS - ROWS):
         fetch(i).start()
 
     @pl.loop(0, SLOTS // 8)
@@ -194,35 +211,36 @@
         for j in range(8):
             acc[s * 8 + j] = jnp.zeros((B, LANES), f32)
 
-    @pl.loop(0, FR)
-    def _(i):
-        for n in range(KP):
-            p_trans[n * B:(n + 1) * B, :] = p_ref[i, n].T
-        pt = p_trans[...]
-        fetch(i).wait()
-
-        @pl.when(i + A_SLOTS - 1 < FR)
-        def _():
-            fetch(i + A_SLOTS - 1).start()
-
-        a = a_buf.at[i % A_SLOTS]
+    @pl.loop(0, FR // ROWS)
+    def _(step):
+        rows = [step * ROWS + r for r in range(ROWS)]
+        for i in rows:
+            fetch(i).wait()
+        for i in rows:
+            @pl.when(i + A_SLOTS - ROWS < FR)
+            def _():
+                fetch(i + A_SLOTS - ROWS).start()
+
         aps, values = {}, {}
-        for u in range(KA + 2 * AHEAD):
-            if u < KA:
-                aps[u] = jnp.dot(a[u], chosen[col[i * KA + u]], preferred_element_type=f32).astype(bf16)
-            if 0 <= u - AHEAD < KA:
-                values[u - AHEAD] = jnp.dot(pt, aps.pop(u - AHEAD), preferred_element_type=f32)
-            k = u - 2 * AHEAD
-            if k < 0:
+        for u in range(ROWS * KA + 2 * AHEAD):
+            if u < ROWS * KA:
+                i, k = rows[u // KA], u % KA
+                aps[u] = jnp.dot(a_buf[i % A_SLOTS, k], chosen[col[i, k]], preferred_element_type=f32).astype(bf16)
+            v = u - AHEAD
+            if 0 <= v < ROWS * KA:
+                values[v] = jnp.dot(p_trans[rows[v // KA]], aps.pop(v), preferred_element_type=f32)
+            w = v - AHEAD
+            if w < 0:
                 continue
-            value = values.pop(k)
+            i, k = rows[w // KA], w % KA
+            value = values.pop(w)
             for n in range(KP):
                 for m in range(KP):
-                    slot = tgt[i * (KP * KA * KP) + n * (KA * KP) + k * KP + m]
+                    slot = tgt[i, n * (KA * KP) + k * KP + m]
                     acc[slot] += value[n * B:(n + 1) * B, m * LANES:(m + 1) * LANES]
 
 
-def products(a_rows, columns, p_rows, chosen, slots):
+def products(a_rows, columns, p_trans, chosen, slots):
     vmem = pl.BlockSpec(memory_space=pltpu.VMEM)
     smem = pl.BlockSpec(memory_space=pltpu.SMEM)
     return pl.pallas_call(
@@ -232,11 +250,10 @@
         out_specs=vmem,
         scratch_shapes=[
             pltpu.VMEM((A_SLOTS, KA, B, B), bf16),
-            pltpu.VMEM((KP * B, B), bf16),
             pltpu.SemaphoreType.DMA((A_SLOTS,))],
-        compiler_params=pltpu.CompilerParams(vmem_limit_bytes=8 << 20),
+        compiler_params=pltpu.CompilerParams(vmem_limit_bytes=10 << 20),
         name="products",
-    )(columns.reshape(-1), slots.reshape(-1), a_rows, p_rows, chosen)
+    )(columns, slots, a_rows, p_trans, chosen)
 
 
 BATCH = 16
@@ -396,7 +413,7 @@
     dma = pltpu.SemaphoreType.DMA
     return pl.pallas_call(
         scatter_kernel,
-        out_shape=jax.ShapeDtypeStruct((1, OWN, B, B), f32),
+        out_shape=pltpu.VMEM((1, OWN, B, B), f32),
         in_specs=[pl.BlockSpec(memory_space=pltpu.VMEM)],
         out_specs=pl.BlockSpec(memory_space=pltpu.VMEM),
         scratch_shapes=[
@@ -412,8 +429,8 @@
 
 
 def shards(a_blocks, col_index, prolong, target):
-    chosen = gather(prolong[0])
-    acc = products(a_blocks[0], col_index[0], prolong[0], chosen, slot_of(target[0]))
+    chosen, p_trans = gather(prolong[0])
+    acc = products(a_blocks[0], col_index[0], p_trans, chosen, slot_of(target[0]))
     return scatter(acc)
 
 

time: 129 us -> 121 us (0.938)
  Pallas kernels: 124 us -> 118 us
  local copies, waits for them, and re-layouts: 4.47 us -> 1.38 us
    pallas_call x1, Pallas kernels: 36.8 us -> 30.6 us  [products(): pl.pallas_call(product_kernel, out_shape=pltpu.VMEM((SLOTS, B, LANES), f3...]
    unnamed x3, local copies, waits for them, and re-layouts: 2.88 us -> 1.38 us
where the time goes in v5:
time: 121 us; the launch traced here: 120 us
  Pallas kernels  118 us (98%)
  local copies, waits for them, and re-layouts  1.38 us (1%)
    pallas_call x1, Pallas kernels, gather(): pl.pallas_call(gather_kernel, out_shape=(jax.ShapeDtypeStruct((FR * MEMBE...  50.4 us
    pallas_call x1, Pallas kernels, scatter(): pl.pallas_call(scatter_kernel, out_shape=pltpu.VMEM((1, OWN, B, B), f32),...  37.3 us
    pallas_call x1, Pallas kernels, products(): pl.pallas_call(product_kernel, out_shape=pltpu.VMEM((SLOTS, B, LANES), f3...  30.6 us

profile of v5, /device:TPU:0, one launch (start us, length us, event | category | flops | bytes accessed | tf_op | source)
XLA Modules:
  0.0 120.4 jit_solution(16485652044529685868)
XLA Ops:
  0.0 0.8 fusion.13.tgt
  0.8 50.4 %gather_prolong.1 = (bf16[192,96,256]{2,1,0:T(8,128)(2,1)S(1)}, bf16[24,192,96]{2,1,0:T(8,128)(2,1)S(1)}) custom-call(bf16[24,2,96,96]{3,2,1,0:T(8,128)(2,1)} %bitcast.23), custom_call_target="tpu_custom_call" | custom-call | tf_op jit(solution)/shard_map/gather_prolong/pallas_call | solution.py:179
  51.2 0.0 copy-start
  51.2 0.7 copy-done
  51.9 30.6 %products.1.acc = f32[512,96,128]{2,1,0:T(8,128)S(1)} custom-call(s32[24,27]{1,0:T(8,128)S(1)} %bitcast.21, s32[24,108]{1,0:T(8,128)S(1)} %fusion.13.tgt, bf16[24,27,96,96]{3,2,1,0:T(8,128)(2,1)} %bitcast.22, bf16[24,192,96]{2,1,0:T(8,128)(2,1)S(1)} %get-tuple-element.7.p_trans, bf16[192,96,256]{2,1,0:T(8,128)(2,1)S(1)} %get-tuple-element.8.chosen), custom_call_target="tpu_custom_call" | custom-call | tf_op jit(solution)/shard_map/products/pallas_call | solution.py:246
  82.5 37.3 %sum_at_owners.1 = f32[1,4,96,96]{3,2,1,0:T(8,128)S(1)} custom-call(f32[512,96,128]{2,1,0:T(8,128)S(1)} %products.1.acc), custom_call_target="tpu_custom_call" | custom-call | tf_op jit(solution)/shard_map/sum_at_owners/pallas_call | solution.py:414
  119.7 0.7 copy.6
Async XLA Ops:
  51.2 0.7 copy-start

commit v6 on v5

--- a/solution.py
+++ b/solution.py
@@ -62,12 +62,13 @@
 
 
 def slot_of(target):
-    owner = target // OWN
-    bits = bits_of(owner // MEMBERS, owner % MEMBERS)
-    index = bits["core"]
-    for bit in BITS:
-        index = index * 2 + bits[bit]
-    return index * OWN + target % OWN
+    blk, grp = target >> 2 & 7, target >> 5
+    zl, zh, xh, yh = blk >> 2, grp >> 1 & 1, blk >> 1 & 1, grp >> 3
+    bits = (grp & 1, xh ^ (blk & 1), yh ^ (grp >> 2 & 1), zh ^ zl, xh, yh, zh)
+    index = bits[0]
+    for bit in bits[1:]:
+        index = index << 1 | bit
+    return index << 2 | target & 3
 
 
 def fold(main, tail):
@@ -103,13 +104,16 @@
     return index, bits["zl"] * 4 + bits["xh"] * 2 + (bits["xh"] + bits["xg"]) % 2
 
 
-def gather_kernel(p_hbm, out_ref, trans_ref, p_ref, landed, load_sem, send_sem, recv_sem):
+def gather_kernel(p_hbm, c_hbm, t_hbm, out_ref, trans_ref, c_ref, s_ref, p_ref, landed, t_ref, table_sem, load_sem, send_sem, recv_sem):
+    tables = [pltpu.make_async_copy(c_hbm, c_ref, table_sem.at[0]), pltpu.make_async_copy(t_hbm, t_ref, table_sem.at[1])]
     loads = []
     for part in range(G_PARTS):
         rows = pl.ds(part * G_ROWS, G_ROWS)
         load = pltpu.make_async_copy(p_hbm.at[rows], p_ref.at[rows], load_sem.at[part])
         load.start()
         loads.append(load)
+    for table in tables:
+        table.start()
     grp, blk = lax.axis_index("grp"), lax.axis_index("blk")
     partners = {bit: partner_of(grp, blk, bit) for bit in G_ORDERS[0]}
     barrier = pltpu.get_barrier_semaphore()
@@ -164,6 +168,10 @@
     def _(r):
         for n in range(KP):
             trans_ref[r, n * B:(n + 1) * B, :] = p_ref[r, n].T
+
+    for table in tables:
+        table.wait()
+    s_ref[...] = slot_of(t_ref[...])
     for flip in range(1, MEMBERS):
         for part in range(G_PARTS):
             arrivals[part, flip].wait_recv()
@@ -175,22 +183,25 @@
         copy.wait_send()
 
 
-def gather(prolong):
+def gather(prolong, columns, targets):
     return pl.pallas_call(
         gather_kernel,
         out_shape=(
             jax.ShapeDtypeStruct((FR * MEMBERS, B, KP * LANES), bf16),
-            jax.ShapeDtypeStruct((FR, KP * B, B), bf16)),
-        in_specs=[pl.BlockSpec(memory_space=pl.ANY)],
-        out_specs=(pl.BlockSpec(memory_space=pltpu.VMEM), pl.BlockSpec(memory_space=pltpu.VMEM)),
+            jax.ShapeDtypeStruct((FR, KP * B, B), bf16),
+            jax.ShapeDtypeStruct(columns.shape, jnp.int32),
+            jax.ShapeDtypeStruct(targets.shape, jnp.int32)),
+        in_specs=[pl.BlockSpec(memory_space=pl.ANY)] * 3,
+        out_specs=(pl.BlockSpec(memory_space=pltpu.VMEM),) * 4,
         scratch_shapes=[
             pltpu.VMEM((FR, KP, B, B), bf16),
             pltpu.VMEM((G_PARTS, MEMBERS, G_ROWS, KP * PACK, LANES), bf16),
-            pltpu.SemaphoreType.DMA((G_PARTS,)),
+            pltpu.VMEM(targets.shape, jnp.int32),
+            pltpu.SemaphoreType.DMA((2,)), pltpu.SemaphoreType.DMA((G_PARTS,)),
             pltpu.SemaphoreType.DMA((G_PARTS, MEMBERS)), pltpu.SemaphoreType.DMA((G_PARTS, MEMBERS))],
         compiler_params=pltpu.CompilerParams(collective_id=0, has_side_effects=True, vmem_limit_bytes=20 << 20),
         name="gather_prolong",
-    )(pltpu.with_memory_space_constraint(prolong, pltpu.HBM))
+    )(*(pltpu.with_memory_space_constraint(v, pltpu.HBM) for v in (prolong, columns, targets)))
 
 
 ROWS = 4
@@ -314,33 +325,36 @@
         pl.semaphore_signal(barrier, inc=1, device_id=device, device_id_type=MESH)
 
     crossed, first, second, third, final = {}, {}, {}, {}, {}
-    def cross_over(part, chunk):
+    def pack(part, chunk):
         offset = (1 - mine[part][0] if chunk == 0 else mine[part][0]) * 32
         fill(cross.at[part, chunk], 32, lambda e: packed(part, 1 - core, offset + e))
-        if chunk == 0 and part == 0:
-            pl.semaphore_wait(barrier, len(flips))
+
+    def cross_over(part, chunk):
         crossed[part, chunk] = send(
             cross.at[part, chunk], other.at[part, chunk], core_send.at[part, chunk], core_recv.at[part, chunk],
             partners[("core",)])
 
-    def give_away(part):
+    def give_away(part, chunk):
+        offset = (1 - mine[part][1] if chunk == 0 else mine[part][1]) * 16
+        away = (1 - mine[part][0]) * 32 + offset
+        fill(give0.at[part, chunk], 16,
+             lambda e: packed(part, core, away + e) + other[part, 0, offset + e].astype(f32))
+        first[part, chunk] = send(
+            give0.at[part, chunk], got0.at[part, chunk], send0.at[part, chunk], recv0.at[part, chunk],
+            partners[(order_of(part)[0],)])
+
+    for part in range(PARTS):
+        pack(part, 0)
+    pl.semaphore_wait(barrier, len(flips))
+    for part in range(PARTS):
+        cross_over(part, 0)
+    for part in range(PARTS):
         crossed[part, 0].wait_recv()
-        for chunk in range(2):
-            offset = (1 - mine[part][1] if chunk == 0 else mine[part][1]) * 16
-            away = (1 - mine[part][0]) * 32 + offset
-            fill(give0.at[part, chunk], 16,
-                 lambda e: packed(part, core, away + e) + other[part, 0, offset + e].astype(f32))
-            first[part, chunk] = send(
-                give0.at[part, chunk], got0.at[part, chunk], send0.at[part, chunk], recv0.at[part, chunk],
-                partners[(order_of(part)[0],)])
-
-    cross_over(0, 0)
-    cross_over(1, 0)
-    for part in range(PARTS):
-        if part + 2 < PARTS:
-            cross_over(part + 2, 0)
-        give_away(part)
-    for part in range(PARTS):
+        give_away(part, 0)
+    for part in range(PARTS):
+        give_away(part, 1)
+    for part in range(PARTS):
+        pack(part, 1)
         cross_over(part, 1)
     for part in range(PARTS):
         crossed[part, 1].wait_recv()
@@ -377,16 +391,17 @@
 
     for part in range(PARTS):
         third[part].wait_recv()
+        values = []
         for r in range(8):
             entry = 0
             for i in range(3):
                 bit = mine[part][3 + i]
                 entry = entry * 2 + (1 - bit if r >> (2 - i) & 1 else bit)
-            value = keep2[part, entry] + got2[part, entry].astype(f32)
-            if r == 0:
-                total[part] = value
-                continue
-            last[part, r - 1] = value.astype(bf16)
+            values.append(keep2[part, entry] + got2[part, entry].astype(f32))
+        total[part] = values[0]
+        for r in range(1, 8):
+            last[part, r - 1] = values[r].astype(bf16)
+        for r in range(1, 8):
             final[part, r] = send(
                 last.at[part, r - 1], arrived.at[part, r - 1], last_send.at[part, r - 1], last_recv.at[part, r - 1],
                 partners[tuple(sorted(direct(part, r)))])
@@ -429,8 +444,8 @@
 
 
 def shards(a_blocks, col_index, prolong, target):
-    chosen, p_trans = gather(prolong[0])
-    acc = products(a_blocks[0], col_index[0], p_trans, chosen, slot_of(target[0]))
+    chosen, p_trans, columns, slots = gather(prolong[0], col_index[0], target[0])
+    acc = products(a_blocks[0], columns, p_trans, chosen, slots)
     return scatter(acc)
 
 

time: 121 us -> 117 us (0.967)
  Pallas kernels: 118 us -> 116 us
    pallas_call x1, Pallas kernels: 37.3 us -> 35.3 us  [scatter(): pl.pallas_call(scatter_kernel, out_shape=pltpu.VMEM((1, OWN, B, B), f32),...]
where the time goes in v6:
time: 117 us
  Pallas kernels  116 us (99%)
    pallas_call x1, Pallas kernels, gather(): pl.pallas_call(gather_kernel, out_shape=(jax.ShapeDtypeStruct((FR * MEMBE...  50.3 us
    pallas_call x1, Pallas kernels, scatter(): pl.pallas_call(scatter_kernel, out_shape=pltpu.VMEM((1, OWN, B, B), f32),...  35.3 us
    pallas_call x1, Pallas kernels, products(): pl.pallas_call(product_kernel, out_shape=pltpu.VMEM((SLOTS, B, LANES), f3...  30.6 us

profile of v6, /device:TPU:0, one launch (start us, length us, event | category | flops | bytes accessed | tf_op | source)
XLA Modules:
  0.0 116.8 jit_solution(18340517843256553747)
XLA Ops:
  0.0 50.3 %gather_prolong.1 = (bf16[192,96,256]{2,1,0:T(8,128)(2,1)S(1)}, bf16[24,192,96]{2,1,0:T(8,128)(2,1)S(1)}, s32[24,27]{1,0:T(8,128)S(1)}, s32[24,108]{1,0:T(8,128)S(1)}) custom-call(bf16[24,2,96,96]{3,2,1,0:T(8,128)(2,1)} %bitcast.5, s32[24,27]{1,0:T(8,128)} %bitcast.6, s32[24,108]{1,0:T(8,128)} %bitcast.7), custom_call_target="tpu_custom_call" | custom-call | tf_op jit(solution)/shard_map/gather_prolong/pallas_call | solution.py:187
  50.3 30.6 %products.1.acc = f32[512,96,128]{2,1,0:T(8,128)S(1)} custom-call(s32[24,27]{1,0:T(8,128)S(1)} %get-tuple-element.9.col, s32[24,108]{1,0:T(8,128)S(1)} %get-tuple-element.10.tgt, bf16[24,27,96,96]{3,2,1,0:T(8,128)(2,1)} %bitcast.4, bf16[24,192,96]{2,1,0:T(8,128)(2,1)S(1)} %get-tuple-element.11.p_trans, bf16[192,96,256]{2,1,0:T(8,128)(2,1)S(1)} %get-tuple-element.12.chosen), custom_call_target="tpu_custom_call" | custom-call | tf_op jit(solution)/shard_map/products/pallas_call | solution.py:257
  80.9 35.3 %sum_at_owners.1 = f32[1,4,96,96]{3,2,1,0:T(8,128)S(1)} custom-call(f32[512,96,128]{2,1,0:T(8,128)S(1)} %products.1.acc), custom_call_target="tpu_custom_call" | custom-call | tf_op jit(solution)/shard_map/sum_at_owners/pallas_call | solution.py:429
  116.1 0.7 copy.6
